TPU v7x, 32 devices: a whole 2x2x4 slice. The times are simulated.
32 devices in a mesh: unit: 2 (over y), row: 16 (over z, x, core).
Axes of the slice: x: 2, y: 2, z: 4, core: 2. Of those that a mesh axis runs over, the one named last changes fastest.
Arguments:
- tokens: bfloat16 [16384, 768], P('row'), may hold values from -5 to 5
- doc_ids: int32 [1, 16384], replicated, may hold values from 0 to 11, never falling along the last dimension, each value on 1 to 4096 neighbouring positions
- valid: int32 [1, 16384], replicated, may hold values from 0 to 1, as said below
- ln1_gain: float32 [768], replicated, may hold values from 0.5 to 1.5
- ln1_shift: float32 [768], replicated, may hold values from -0.3 to 0.3
- w_query: bfloat16 [768, 768], P(None, 'unit'), may hold values from -0.21875 to 0.21875
- b_query: float32 [768], P('unit'), may hold values from -3 to 3
- w_key: bfloat16 [768, 768], P(None, 'unit'), may hold values from -0.21875 to 0.21875
- w_value: bfloat16 [768, 768], P(None, 'unit'), may hold values from -0.21875 to 0.21875
- b_value: float32 [768], P('unit'), may hold values from -0.3 to 0.3
- w_out: bfloat16 [768, 768], P('unit'), may hold values from -1.75 to 1.75
- b_out: float32 [768], replicated, may hold values from -1.2 to 1.2
- ln2_gain: float32 [768], replicated, may hold values from 0.5 to 1.5
- ln2_shift: float32 [768], replicated, may hold values from -0.6 to 0.6
- w_up: bfloat16 [768, 3072], P(None, 'unit'), may hold values from -0.21875 to 0.21875
- b_up: float32 [3072], P('unit'), may hold values from -3 to 3
- w_down: bfloat16 [3072, 768], P('unit'), may hold values from -0.109375 to 0.109375
- b_down: float32 [768], replicated, may hold values from -1.2 to 1.2
- cotangent: bfloat16 [16384, 768], P('row'), may hold values from -5 to 5
Outputs:
- mixed_out: bfloat16 [16384, 768], P('row')
- grad_tokens: float32 [16384, 768], P('row')
- grad_ln1_gain: float32 [768], replicated
- grad_ln1_shift: float32 [768], replicated
- grad_w_query: float32 [768, 768], P(None, 'unit')
- grad_b_query: float32 [768], P('unit')
- grad_w_key: float32 [768, 768], P(None, 'unit')
- grad_w_value: float32 [768, 768], P(None, 'unit')
- grad_b_value: float32 [768], P('unit')
- grad_w_out: float32 [768, 768], P('unit')
- grad_b_out: float32 [768], replicated
- grad_ln2_gain: float32 [768], replicated
- grad_ln2_shift: float32 [768], replicated
- grad_w_up: float32 [768, 3072], P(None, 'unit')
- grad_b_up: float32 [3072], P('unit')
- grad_w_down: float32 [3072, 768], P('unit')
- grad_b_down: float32 [768], replicated
Inputs may be any that keep to these rules, and one draw needn't show every extreme that they name: `valid`: every sequence but the last is all ones; the last ends in a run of 2048 to 8192 zeros.
All inputs are finite; a program needn't handle non-finite values.
Results may differ from a plain program's by a relative error of at most 0.012.
The roundings to bfloat16 on the way count: a program that leaves them out, or rounds other values in their place, can miss the bound.
Values may be sent and summed in bfloat16 or wider, within the bound.
No kernel may reach another device: no remote copies, remote signals or barrier semaphores. Data moves between devices by JAX's collectives and lax.ppermute only.
A program may use at most 256 MiB of HBM per device.

v0:
```python
from functools import reduce
import math

import jax
import jax.numpy as jnp
from jax import lax
from jax.sharding import PartitionSpec as P

HEAD_DIM = 48
SEG0 = 1024
BRANCHES = 5


EPSILON = 1e-05
MASKED = -1000000000.0
GELU_SCALE = 0.7978845608028654


def partner(value, axis, bit):
    mask = 2**bit
    pairs = [(source, source ^ mask) for source in range(lax.axis_size(axis))]
    return lax.ppermute(value, axis, pairs)


def layer_norm(values, norm_gain, norm_shift):
    row_mean = jnp.mean(values, axis=-1, keepdims=True)
    centred = values - row_mean
    row_var = jnp.mean(centred * centred, axis=-1, keepdims=True)
    return centred * lax.rsqrt(row_var + EPSILON) * norm_gain + norm_shift


def gelu_tanh(values):
    cubic = values + 0.044715 * values * values * values
    return 0.5 * values * (1.0 + jnp.tanh(GELU_SCALE * cubic))


def pick_rows(values, stride, offsets):
    count = offsets.shape[0]
    shaped = values.reshape((values.shape[0] // stride, stride) + values.shape[1:])
    chosen_mask = (jnp.arange(stride)[:, None] == offsets[None, :]).reshape(
        (1, stride, count) + (1,) * (values.ndim - 2)
    )
    chosen = jnp.sum(
        jnp.where(chosen_mask, shaped, jnp.zeros((), values.dtype)), axis=1, dtype=values.dtype
    )
    return jnp.moveaxis(chosen, 1, 0)


def spread_rows(values, stride, offsets):
    count = offsets.shape[0]
    moved = jnp.moveaxis(values, 0, 1)
    chosen_mask = (jnp.arange(stride)[:, None] == offsets[None, :]).reshape(
        (1, stride, count) + (1,) * (values.ndim - 2)
    )
    full_rows = jnp.where(chosen_mask, moved[:, None], jnp.zeros((), values.dtype))
    return full_rows.reshape((moved.shape[0] * stride,) + moved.shape[1:])


def blockwise(kernel, operands, unit_count, row_count):
    block_size = math.gcd(unit_count, max(1, 512 // row_count))
    split_parts = tuple(
        (item.reshape((unit_count // block_size, block_size) + item.shape[1:]) for item in operands)
    )
    results = lax.map(lambda group_parts: kernel(*group_parts), split_parts)
    return tuple((item.reshape((unit_count,) + item.shape[2:]) for item in results))


def masked_scores(queries, key_units, query_tags, key_tags):
    scores = jnp.einsum("uqd,ukd->uqk", queries, key_units, preferred_element_type=jnp.float32)
    return jnp.where(query_tags[:, :, None] == key_tags[:, None, :], scores, MASKED)


def attend_block(queries, key_units, value_units, query_tags, key_tags):
    scores = masked_scores(queries, key_units, query_tags, key_tags)
    row_peak = jnp.max(scores, axis=-1, keepdims=True)
    weights = jnp.exp(scores - row_peak)
    weight_sum = jnp.sum(weights, axis=-1, keepdims=True)
    attn_probs = (weights / weight_sum).astype(jnp.bfloat16)
    outputs = jnp.einsum(
        "uqk,ukd->uqd", attn_probs, value_units, preferred_element_type=jnp.float32
    )
    return (outputs, row_peak[..., 0] + jnp.log(weight_sum[..., 0]))


def both_grads_block(
    queries, key_units, value_units, query_tags, key_tags, log_total, out_grad, lse_grad
):
    attn_probs = jnp.exp(
        masked_scores(queries, key_units, query_tags, key_tags) - log_total[:, :, None]
    )
    prob_grad = jnp.einsum(
        "uqd,ukd->uqk", out_grad, value_units, preferred_element_type=jnp.float32
    )
    inner_sum = jnp.sum(attn_probs * prob_grad, axis=-1, keepdims=True)
    score_grad = (attn_probs * (prob_grad - inner_sum + lse_grad[:, :, None])).astype(jnp.bfloat16)
    query_grad = jnp.einsum(
        "uqk,ukd->uqd", score_grad, key_units, preferred_element_type=jnp.float32
    )
    key_grad = jnp.einsum("uqk,uqd->ukd", score_grad, queries, preferred_element_type=jnp.float32)
    value_grad = jnp.einsum(
        "uqk,uqd->ukd",
        attn_probs.astype(jnp.bfloat16),
        out_grad,
        preferred_element_type=jnp.float32,
    )
    return (query_grad, key_grad, value_grad)


def double_up(blocks, levels, row_pos, sender):
    blocks = list(blocks)
    for bit_level in range(max(levels)):
        active = [member for member in range(len(blocks)) if levels[member] > bit_level]
        lengths = [blocks[member].shape[2] for member in active]
        joined = jnp.concatenate([blocks[member] for member in active], axis=2)
        received = sender(joined, bit_level)
        upper_half = row_pos >> bit_level & 1 == 1
        offset_at = 0
        for member, length in zip(active, lengths):
            theirs = lax.slice_in_dim(received, offset_at, offset_at + length, axis=2)
            own_part = blocks[member]
            blocks[member] = jnp.where(
                upper_half,
                jnp.concatenate([theirs, own_part], axis=2),
                jnp.concatenate([own_part, theirs], axis=2),
            )
            offset_at += length
    return blocks


def halve_down(blocks, levels, row_pos, sender):
    blocks = list(blocks)
    for bit_level in reversed(range(max(levels))):
        active = [member for member in range(len(blocks)) if levels[member] > bit_level]
        upper_half = row_pos >> bit_level & 1 == 1
        kept_parts = []
        sent_parts = []
        for member in active:
            half_len = blocks[member].shape[2] // 2
            lower_part = blocks[member][:, :, :half_len]
            upper_part = blocks[member][:, :, half_len:]
            kept_parts.append(jnp.where(upper_half, upper_part, lower_part))
            sent_parts.append(jnp.where(upper_half, lower_part, upper_part))
        received = sender(jnp.concatenate(sent_parts, axis=2), bit_level)
        offset_at = 0
        for member, kept_part in zip(active, kept_parts):
            length = kept_part.shape[2]
            blocks[member] = kept_part + lax.slice_in_dim(
                received, offset_at, offset_at + length, axis=2
            )
            offset_at += length
    return blocks


def local(
    tokens,
    doc_ids,
    valid,
    ln1_gain,
    ln1_shift,
    w_query,
    b_query,
    w_key,
    w_value,
    b_value,
    w_out,
    b_out,
    ln2_gain,
    ln2_shift,
    w_up,
    b_up,
    w_down,
    b_down,
    cotangent,
):
    rows_here = tokens.shape[0]
    local_width = w_query.shape[1]
    heads_here = local_width // HEAD_DIM
    scaling = HEAD_DIM ** (-0.5)
    unit_pos = lax.axis_index("unit")
    row_pos = lax.axis_index("row")
    head_ids = unit_pos * heads_here + jnp.arange(heads_here, dtype=jnp.int32)
    all_tags = jnp.where(valid == 1, doc_ids, -1).reshape(-1)
    own_tags = lax.dynamic_slice_in_dim(all_tags, row_pos * rows_here, rows_here)
    residual = tokens.astype(jnp.float32)
    normed = layer_norm(residual, ln1_gain, ln1_shift)
    normed_low = normed.astype(jnp.bfloat16)
    head_shape = (rows_here, heads_here, HEAD_DIM)
    query_all = (
        ((jnp.dot(normed_low, w_query, preferred_element_type=jnp.float32) + b_query) * scaling)
        .astype(jnp.bfloat16)
        .reshape(head_shape)
    )
    key_all = (
        jnp.dot(normed_low, w_key, preferred_element_type=jnp.float32)
        .astype(jnp.bfloat16)
        .reshape(head_shape)
    )
    value_all = (
        (jnp.dot(normed_low, w_value, preferred_element_type=jnp.float32) + b_value)
        .astype(jnp.bfloat16)
        .reshape(head_shape)
    )
    branch_plans = []
    for branch in range(BRANCHES):
        stride = 2**branch
        extent = SEG0 * stride
        group_size = max(1, extent // rows_here)
        branch_plans.append(
            (
                stride,
                group_size,
                group_size.bit_length() - 1,
                max(1, rows_here // extent),
                head_ids % stride,
            )
        )
    levels = [branch_plan[2] for branch_plan in branch_plans]
    local_kv = [
        jnp.stack(
            [
                pick_rows(key_all, branch_plan[0], branch_plan[4]),
                pick_rows(value_all, branch_plan[0], branch_plan[4]),
            ]
        )
        for branch_plan in branch_plans
    ]

    def send_pairs(joined, bit_level):
        return partner(joined, "row", bit_level)

    gathered = double_up(local_kv, levels, row_pos, send_pairs)
    saved_parts = []
    branch_outs = []
    branch_lses = []
    selections = []
    for branch in range(BRANCHES):
        stride, group_size, branch_levels, segments, offsets = branch_plans[branch]
        unit_count = heads_here * segments
        per_unit = rows_here // stride // segments
        block_start = row_pos // group_size * (group_size * rows_here)
        block_tags = lax.dynamic_slice_in_dim(all_tags, block_start, group_size * rows_here)
        key_tags = pick_rows(
            jnp.broadcast_to(block_tags[:, None], (group_size * rows_here, heads_here)),
            stride,
            offsets,
        )
        query_tags = pick_rows(
            jnp.broadcast_to(own_tags[:, None], (rows_here, heads_here)), stride, offsets
        )
        queries = pick_rows(query_all, stride, offsets)
        key_units = gathered[branch][0]
        value_units = gathered[branch][1]
        outputs, log_total = blockwise(
            attend_block,
            (queries, key_units, value_units, query_tags, key_tags),
            unit_count,
            per_unit,
        )
        saved_parts.append((queries, key_units, value_units, query_tags, key_tags, log_total))
        branch_outs.append(spread_rows(outputs, stride, offsets))
        branch_lses.append(spread_rows(log_total, stride, offsets))
        selections.append(jnp.arange(rows_here)[:, None] % stride == offsets[None, :])
    peak_lse = reduce(
        jnp.maximum,
        [
            jnp.where(mask_here, lse_here, MASKED)
            for mask_here, lse_here in zip(selections, branch_lses)
        ],
    )
    weights = [
        jnp.where(mask_here, jnp.exp(jnp.where(mask_here, lse_here, peak_lse) - peak_lse), 0.0)
        for mask_here, lse_here in zip(selections, branch_lses)
    ]
    weight_sum = reduce(jnp.add, weights)
    shares = [weight_here / weight_sum for weight_here in weights]
    merged = reduce(
        jnp.add,
        [share_here[:, :, None] * out_here for share_here, out_here in zip(shares, branch_outs)],
    )
    merged_low = merged.reshape(rows_here, local_width).astype(jnp.bfloat16)
    attention = (
        lax.psum(jnp.dot(merged_low, w_out, preferred_element_type=jnp.float32), "unit") + b_out
    )
    middle = residual + attention
    normed2 = layer_norm(middle, ln2_gain, ln2_shift)
    normed2_low = normed2.astype(jnp.bfloat16)
    up_input = jnp.dot(normed2_low, w_up, preferred_element_type=jnp.float32) + b_up
    hidden_low = gelu_tanh(up_input).astype(jnp.bfloat16)
    feed_out = (
        lax.psum(jnp.dot(hidden_low, w_down, preferred_element_type=jnp.float32), "unit") + b_down
    )
    mixed_out = (middle + feed_out).astype(jnp.bfloat16)
    back_rows = cotangent.astype(jnp.float32)
    grad_b_down = jnp.sum(back_rows, axis=0)
    grad_w_down = jnp.einsum("tf,td->fd", hidden_low, cotangent, preferred_element_type=jnp.float32)
    hidden_grad = jnp.einsum("td,fd->tf", cotangent, w_down, preferred_element_type=jnp.float32)
    _, gelu_pull = jax.vjp(gelu_tanh, up_input)
    up_grad_low = gelu_pull(hidden_grad)[0].astype(jnp.bfloat16)
    grad_b_up = jnp.sum(up_grad_low.astype(jnp.float32), axis=0)
    grad_w_up = jnp.einsum(
        "tc,tf->cf", normed2_low, up_grad_low, preferred_element_type=jnp.float32
    )
    normed2_grad = lax.psum(
        jnp.einsum("tf,cf->tc", up_grad_low, w_up, preferred_element_type=jnp.float32), "unit"
    )
    _, norm2_pull = jax.vjp(layer_norm, middle, ln2_gain, ln2_shift)
    middle_part, grad_ln2_gain, grad_ln2_shift = norm2_pull(normed2_grad)
    middle_grad = back_rows + middle_part
    attention_grad = middle_grad.astype(jnp.bfloat16)
    grad_b_out = jnp.sum(attention_grad.astype(jnp.float32), axis=0)
    grad_w_out = jnp.einsum(
        "tc,td->cd", merged_low, attention_grad, preferred_element_type=jnp.float32
    )
    merged_grad = jnp.einsum(
        "td,cd->tc", attention_grad, w_out, preferred_element_type=jnp.float32
    ).reshape(head_shape)
    share_grads = [jnp.sum(merged_grad * out_here, axis=-1) for out_here in branch_outs]
    mean_grad = reduce(
        jnp.add, [share_here * grad_here for share_here, grad_here in zip(shares, share_grads)]
    )
    out_grad_units = []
    lse_grad_units = []
    for branch in range(BRANCHES):
        stride, group_size, branch_levels, segments, offsets = branch_plans[branch]
        unit_count = heads_here * segments
        per_unit = rows_here // stride // segments
        out_grad_rows = (shares[branch][:, :, None] * merged_grad).astype(jnp.bfloat16)
        lse_grad_rows = shares[branch] * (share_grads[branch] - mean_grad)
        out_grad_units.append(pick_rows(out_grad_rows, stride, offsets))
        lse_grad_units.append(pick_rows(lse_grad_rows, stride, offsets))
    query_grad = jnp.zeros(head_shape, jnp.float32)
    key_grad = jnp.zeros(head_shape, jnp.float32)
    value_grad = jnp.zeros(head_shape, jnp.float32)
    returned = []
    for branch in range(BRANCHES):
        stride, group_size, branch_levels, segments, offsets = branch_plans[branch]
        unit_count = heads_here * segments
        per_unit = rows_here // stride // segments
        queries, key_units, value_units, query_tags, key_tags, log_total = saved_parts[branch]
        grad_q, grad_k, grad_v = blockwise(
            both_grads_block,
            (
                queries,
                key_units,
                value_units,
                query_tags,
                key_tags,
                log_total,
                out_grad_units[branch],
                lse_grad_units[branch],
            ),
            unit_count,
            per_unit,
        )
        query_grad = query_grad + spread_rows(grad_q, stride, offsets)
        returned.append(jnp.stack([grad_k, grad_v]))

    def send_grads(joined, bit_level):
        return partner(joined, "row", bit_level)

    returned = halve_down(returned, levels, row_pos, send_grads)
    for branch in range(BRANCHES):
        stride, group_size, branch_levels, segments, offsets = branch_plans[branch]
        key_grad = key_grad + spread_rows(returned[branch][0], stride, offsets)
        value_grad = value_grad + spread_rows(returned[branch][1], stride, offsets)
    query_low = query_grad.reshape(rows_here, local_width).astype(jnp.bfloat16)
    key_low = key_grad.reshape(rows_here, local_width).astype(jnp.bfloat16)
    value_low = value_grad.reshape(rows_here, local_width).astype(jnp.bfloat16)
    grad_b_query = scaling * jnp.sum(query_low.astype(jnp.float32), axis=0)
    grad_w_query = scaling * jnp.einsum(
        "tc,tk->ck", normed_low, query_low, preferred_element_type=jnp.float32
    )
    grad_w_key = jnp.einsum("tc,tk->ck", normed_low, key_low, preferred_element_type=jnp.float32)
    grad_w_value = jnp.einsum(
        "tc,tk->ck", normed_low, value_low, preferred_element_type=jnp.float32
    )
    grad_b_value = jnp.sum(value_low.astype(jnp.float32), axis=0)
    normed_part = (
        scaling * jnp.einsum("tk,ck->tc", query_low, w_query, preferred_element_type=jnp.float32)
        + jnp.einsum("tk,ck->tc", key_low, w_key, preferred_element_type=jnp.float32)
        + jnp.einsum("tk,ck->tc", value_low, w_value, preferred_element_type=jnp.float32)
    )
    normed_grad = lax.psum(normed_part, "unit")
    _, norm1_pull = jax.vjp(layer_norm, residual, ln1_gain, ln1_shift)
    input_part, grad_ln1_gain, grad_ln1_shift = norm1_pull(normed_grad)
    grad_tokens = middle_grad + input_part
    (
        grad_ln1_gain,
        grad_ln1_shift,
        grad_w_query,
        grad_b_query,
        grad_w_key,
        grad_w_value,
        grad_b_value,
        grad_w_out,
        grad_b_out,
        grad_ln2_gain,
        grad_ln2_shift,
        grad_w_up,
        grad_b_up,
        grad_w_down,
        grad_b_down,
    ) = lax.psum(
        (
            grad_ln1_gain,
            grad_ln1_shift,
            grad_w_query,
            grad_b_query,
            grad_w_key,
            grad_w_value,
            grad_b_value,
            grad_w_out,
            grad_b_out,
            grad_ln2_gain,
            grad_ln2_shift,
            grad_w_up,
            grad_b_up,
            grad_w_down,
            grad_b_down,
        ),
        "row",
    )
    return (
        mixed_out,
        grad_tokens,
        grad_ln1_gain,
        grad_ln1_shift,
        grad_w_query,
        grad_b_query,
        grad_w_key,
        grad_w_value,
        grad_b_value,
        grad_w_out,
        grad_b_out,
        grad_ln2_gain,
        grad_ln2_shift,
        grad_w_up,
        grad_b_up,
        grad_w_down,
        grad_b_down,
    )


def solution(mesh):
    placed = (
        P("row", None),
        P(),
        P(),
        P(),
        P(),
        P(None, "unit"),
        P("unit"),
        P(None, "unit"),
        P(None, "unit"),
        P("unit"),
        P("unit", None),
        P(),
        P(),
        P(),
        P(None, "unit"),
        P("unit"),
        P("unit", None),
        P(),
        P("row", None),
    )
    return jax.shard_map(
        local,
        mesh=mesh,
        in_specs=placed,
        out_specs=(
            P("row", None),
            P("row", None),
            P(),
            P(),
            P(None, "unit"),
            P("unit"),
            P(None, "unit"),
            P(None, "unit"),
            P("unit"),
            P("unit", None),
            P(),
            P(),
            P(),
            P(None, "unit"),
            P("unit"),
            P("unit", None),
            P(),
        ),
        check_vma=False,
    )
```

profile of v0, /device:TPU:1, one launch (start us, length us, event | category | flops | bytes accessed | tf_op | source)
XLA Modules:
  0.0 1636.3 jit_solution(4865163866600843898)
XLA Ops:
  73.3 6.3 select_reduce_fusion.2
  81.6 6.9 select_reduce_fusion.10
  104.9 48.8 %while.117 = (s32[]{:T(128)}, f32[8,1,1024,48]{2,3,1,0:T(8,128)}, f32[8,1,1024]{2,1,0:T(1,128)}, s32[8,1,1024]{2,1,0:T(1,128)S(1)}, bf16[8,1,1024,48]{3,2,1,0:T(...) while((s32[]{:T(128)}, f32[8,1,1024,48]{2,3,1,0:T(8,128)}, ...), condition=%wide.region_5.6_spmd, body=%wide.region_2.5_spmd.sunk | while | flops 213908480 | bytes 13637733 | solution.py:64
  204.7 41.3 %while.118 = (s32[]{:T(128)}, f32[8,1,512,48]{2,3,1,0:T(8,128)}, f32[8,1,512]{2,1,0:T(1,128)S(1)}, s32[8,1,512]{2,1,0:T(1,128)}, s32[8,1,1024]{2,1,0:T(1,128)S(1...) while((s32[]{:T(128)}, f32[8,1,512,48]{2,3,1,0:T(8,128)}, ...), condition=%wide.region_20.21_spmd, body=%wide.region_17.20_spmd.sunk | while | flops 106954240 | bytes 7098481 | solution.py:64
  274.1 25.6 %while.119 = (s32[]{:T(128)}, f32[4,2,256,48]{2,3,1,0:T(8,128)}, f32[4,2,256]{2,1,0:T(2,128)}, s32[4,2,256]{2,1,0:T(2,128)}, s32[4,2,1024]{2,1,0:T(2,128)}, /*in...) while((s32[]{:T(128)}, f32[4,2,256,48]{2,3,1,0:T(8,128)}, ...), condition=%wide.region_27.28_spmd, body=%wide.region_24.27_spmd.sunk | while | flops 106954240 | bytes 6901873 | solution.py:64
  327.0 6.5 while.120
  347.9 14.2 collective-permute-done.3
  391.0 84.6 %all-reduce.8.cloned.1.call-done = f32[1024,768]{1,0:T(8,128)} async-done(((f32[1024,768]{1,0:T(8,128)}), f32[1024,768]{1,0:T(8,128)}) %all-reduce.8.cloned.1.call-update) | async-done | bytes 3145744 | tf_op jit(solution)/shard_map/psum | solution.py:282
  484.1 10.3 convert_reduce_fusion
  567.3 19.0 %all-reduce.10.cloned.1.call-done = f32[1024,768]{1,0:T(8,128)} async-done(((f32[1024,768]{1,0:T(8,128)}), f32[1024,768]{1,0:T(8,128)}) %all-reduce.10.cloned.1.call-update) | async-done | bytes 3145744 | tf_op jit(solution)/shard_map/psum | solution.py:303
  636.7 6.9 select_reduce_fusion.13
  646.6 7.1 fusion.290
  666.1 62.3 %while.123 = (s32[]{:T(128)}, f32[4,2,256,48]{2,3,1,0:T(8,128)}, f32[4,2,1024,48]{2,3,1,0:T(8,128)}, f32[4,2,1024,48]{2,3,1,0:T(8,128)}, s32[4,2,256]{2,1,0:T(2,...) while((s32[]{:T(128)}, f32[4,2,256,48]{2,3,1,0:T(8,128)}, ...), condition=%wide.region_64.65_spmd, body=%wide.region_62.64_spmd.sunk | while | flops 259001344 | bytes 25576620 | solution.py:64
  732.5 25.7 %while.124 = (s32[]{:T(128)}, f32[2,4,128,48]{2,3,1,0:T(8,128)}, f32[2,4,1024,48]{2,3,1,0:T(8,128)}, f32[2,4,1024,48]{2,3,1,0:T(8,128)}, s32[2,4,128]{2,1,0:T(4,...) while((s32[]{:T(128)}, f32[2,4,128,48]{2,3,1,0:T(8,128)}, ...), condition=%wide.region_69.70_spmd, body=%wide.region_67.69_spmd.sunk | while | flops 259001344 | bytes 26190992 | solution.py:64
  771.3 6.4 select_reduce_fusion.14
  784.7 36.8 %collective-permute-done.5 = f32[2,8,768,48]{2,3,1,0:T(8,128)} collective-permute-done((f32[2,8,768,48]{2,3,1,0:T(8,128)}, f32[2,8,768,48]{2,3,1,0:T(8,128)}, u32[]{:S(2)}, u32[]{:S(2)}) %collective-permute-start.5) | collective-permute-done | bytes 2359328 | tf_op jit(solution)/shard_map/ppermute | solution.py:22
  832.1 92.4 %while.122 = (s32[]{:T(128)}, f32[8,1,512,48]{2,3,1,0:T(8,128)}, f32[8,1,1024,48]{2,3,1,0:T(8,128)}, f32[8,1,1024,48]{2,3,1,0:T(8,128)}, s32[8,1,512]{2,1,0:T(1,...) while((s32[]{:T(128)}, f32[8,1,512,48]{2,3,1,0:T(8,128)}, ...), condition=%wide.region_59.60_spmd, body=%wide.region_57.59_spmd.sunk | while | flops 256900608 | bytes 17570960 | solution.py:64
  941.3 119.7 %while.121 = (s32[]{:T(128)}, f32[8,1,1024,48]{2,3,1,0:T(8,128)}, f32[8,1,1024,48]{2,3,1,0:T(8,128)}, f32[8,1,1024,48]{2,3,1,0:T(8,128)}, s32[8,1,1024]{2,1,0:T(...) while((s32[]{:T(128)}, f32[8,1,1024,48]{2,3,1,0:T(8,128)}, ...), condition=%wide.region_54.55_spmd, body=%wide.region_52.54_spmd.sunk | while | flops 520092672 | bytes 33629320 | solution.py:64
  1182.3 11.1 fusion.277
  1201.0 7.7 fusion.472
  1252.3 7.5 convert_reduce_fusion.4
  1260.0 90.1 %all-reduce.14.cloned.1.call-done = (f32[1024,768]{1,0:T(8,128)}, f32[1024,768]{1,0:T(8,128)}) async-done(((f32[1024,768]{1,0:T(8,128)}, f32[1024,768]{1,0:T(8,128)}), (f32[1024,768]{1,0:T(8,128)}, f32[1024,768]{1,0:T(8,128)})) %all-reduce.14.cloned.1.call-update) | async-done | bytes 6291472 | tf_op jit(solution)/shard_map/psum | solution.py:290
  1358.3 60.4 %all-reduce = (f32[768]{0:T(1024)}, f32[768]{0:T(1024)}, f32[384]{0:T(512)}, f32[384]{0:T(512)}, f32[768]{0:T(1024)}, /*index=5*/f32[768]{0:T(1024)}, f32[768]{0:T(1024)}, f32[1536]{0:T(1024)}, f32[768]{0:T(1024)}) all-reduce(f32[768]{0:T(1024)S(1)} %get-tuple-element.871, ...), channel_id=1, replica_groups=mesh['unit'=2,'row'=16] {'row'}, use_global_device_ids=true, to_apply=%region_77.78 | all-reduce | flops 6912 | bytes 55296 | tf_op jit(solution)/shard_map/psum | solution.py:403
  1423.2 194.2 %all-reduce.12.cloned.1.call-done = (f32[768,384]{1,0:T(8,128)}, f32[768,384]{1,0:T(8,128)}, f32[768,384]{1,0:T(8,128)}, f32[384,768]{1,0:T(8,128)}, f32[768,1536]{1,0:T(8,128)}, /*index=5*/f32[1536,768]{1,0:T(8,128)}) async-done(((f32[768,384]{1,0:T(8,128)}, f32[768,384]{1,0:T(8,128)}, f32[768,384]{1,0:T(8,128)}, f32[384,768]{1,0:T(8,128)}, f32[768,1536]{1,0:T(8,128)}, /*index=5*/f32[1536,768]{1,0:T(8,128)}), ...) | async-done | bytes 14155792 | tf_op jit(solution)/shard_map/psum | solution.py:403
  (1228 shorter events, 1048.6 us)
Async XLA Ops:
  7.2 476.9 %copy-start = (bf16[1536,768]{1,0:T(8,128)(2,1)S(1)}, bf16[1536,768]{1,0:T(8,128)(2,1)}, u32[]{:S(2)}) copy-start(bf16[1536,768]{1,0:T(8,128)(2,1)} %param.51) | copy-start | bytes 7077892
  7.2 468.4 %all-reduce.8.cloned.1.call-start = ((), (), s32[]{:S(2)}) async-start(), calls=%async_computation | async-start | bytes 6291456 | tf_op jit(solution)/shard_map/psum | solution.py:282
  58.4 104.0 %copy-start.202 = (pred[2,8]{1,0:T(4,128)(4,1)}, pred[2,8]{1,0:T(4,128)(4,1)S(1)}, u32[]{:S(2)}) copy-start(pred[2,8]{1,0:T(4,128)(4,1)S(1)} %iota_compare_fusion.3) | copy-start | bytes 52
  58.5 99.0 %copy-start.204 = (pred[4,8]{1,0:T(4,128)(4,1)}, pred[4,8]{1,0:T(4,128)(4,1)S(1)}, u32[]{:S(2)}) copy-start(pred[4,8]{1,0:T(4,128)(4,1)S(1)} %iota_compare_fusion.2) | copy-start | bytes 100
  58.5 95.2 %copy-start.200 = (pred[8,8]{1,0:T(8,128)(4,1)}, pred[8,8]{1,0:T(8,128)(4,1)S(1)}, u32[]{:S(2)}) copy-start(pred[8,8]{1,0:T(8,128)(4,1)S(1)} %iota_compare_fusion.1) | copy-start | bytes 196
  58.5 95.2 %copy-start.173 = (pred[16,8]{1,0:T(8,128)(4,1)}, pred[16,8]{1,0:T(8,128)(4,1)S(1)}, u32[]{:S(2)}) copy-start(pred[16,8]{1,0:T(8,128)(4,1)S(1)} %iota_compare_fusion) | copy-start | bytes 388
  95.1 89.0 %collective-permute-start = (bf16[2,8,960,48]{2,3,1,0:T(8,128)(2,1)}, bf16[2,8,960,48]{2,3,1,0:T(8,128)(2,1)}, u32[]{:S(2)}, u32[]{:S(2)}) collective-permute-start(bf16[2,8,960,48]{2,3,1,0:T(8,128)(2,1)} %maximum_maximum_fusion), channel_id=1, source_target_pairs={{0,1},{1,0},{2,3},{3,2},{4,5},{5,4},{6,7},{7,6},{8,9},{9,8},{10,11... | collective-permute-start | bytes 4423688 | tf_op jit(solution)/shard_map/ppermute | solution.py:22
  156.2 439.3 %copy-start.144 = (pred[1024,8]{0,1:T(8,128)(4,1)}, pred[1024,8]{0,1:T(8,128)(4,1)S(1)}, u32[]{:S(2)}) copy-start(pred[1024,8]{0,1:T(8,128)(4,1)S(1)} %broadcast_in_dim.1189) | copy-start | bytes 24580
  156.5 439.0 %copy-start.146 = (pred[1024,8]{0,1:T(8,128)(4,1)}, pred[1024,8]{0,1:T(8,128)(4,1)S(1)}, u32[]{:S(2)}) copy-start(pred[1024,8]{0,1:T(8,128)(4,1)S(1)} %copy.577) | copy-start | bytes 24580
  198.3 67.1 %collective-permute-start.1 = (bf16[2,8,896,48]{2,3,1,0:T(8,128)(2,1)}, bf16[2,8,896,48]{2,3,1,0:T(8,128)(2,1)}, u32[]{:S(2)}, u32[]{:S(2)}) collective-permute-start(bf16[2,8,896,48]{2,3,1,0:T(8,128)(2,1)} %pad_maximum_fusion.7), channel_id=1, source_target_pairs={{0,2},{1,3},{2,0},{3,1},{4,6},{5,7},{6,4},{7,5},{8,10},{9,11},{10,... | collective-permute-start | bytes 4128776 | tf_op jit(solution)/shard_map/ppermute | solution.py:22
  272.0 47.8 %collective-permute-start.2 = (bf16[2,8,768,48]{2,3,1,0:T(8,128)(2,1)}, bf16[2,8,768,48]{2,3,1,0:T(8,128)(2,1)}, u32[]{:S(2)}, u32[]{:S(2)}) collective-permute-start(bf16[2,8,768,48]{2,3,1,0:T(8,128)(2,1)} %pad_maximum_fusion.8), channel_id=1, source_target_pairs={{0,4},{1,5},{2,6},{3,7},{4,0},{5,1},{6,2},{7,3},{8,12},{9,13},{10,... | collective-permute-start | bytes 3538952 | tf_op jit(solution)/shard_map/ppermute | solution.py:22
  324.7 37.4 %collective-permute-start.3 = (bf16[2,8,512,48]{2,3,1,0:T(8,128)(2,1)}, bf16[2,8,512,48]{2,3,1,0:T(8,128)(2,1)}, u32[]{:S(2)}, u32[]{:S(2)}) collective-permute-start(bf16[2,8,512,48]{2,3,1,0:T(8,128)(2,1)} %maximum_select_fusion.6), channel_id=1, source_target_pairs={{0,8},{1,9},{2,10},{3,11},{4,12},{5,13},{6,14},{7,15},{8,0},{9,1},... | collective-permute-start | bytes 2359304 | tf_op jit(solution)/shard_map/ppermute | solution.py:22
  390.5 85.1 %copy-start.233 = (f32[768]{0:T(1024)S(1)}, f32[768]{0:T(1024)}, u32[]{:S(2)}) copy-start(f32[768]{0:T(1024)} %param.46) | copy-start | bytes 9220
  390.5 195.8 %all-reduce.10.cloned.1.call-start = ((), (), s32[]{:S(2)}) async-start(), calls=%async_computation.1 | async-start | bytes 6291456 | tf_op jit(solution)/shard_map/psum | solution.py:303
  500.4 849.7 %all-reduce.14.cloned.1.call-start = ((), (), s32[]{:S(2)}) async-start(), calls=%async_computation.3 | async-start | bytes 12582912 | tf_op jit(solution)/shard_map/psum | solution.py:290
  656.8 108.1 %collective-permute-start.4 = (f32[2,8,512,48]{2,3,1,0:T(8,128)}, f32[2,8,512,48]{2,3,1,0:T(8,128)}, u32[]{:S(2)}, u32[]{:S(2)}) collective-permute-start(f32[2,8,512,48]{2,3,1,0:T(8,128)} %broadcast_select_fusion), channel_id=1, source_target_pairs={{0,8},{1,9},{2,10},{3,11},{4,12},{5,13},{6,14},{7,15},{8,0},{9,1},... | collective-permute-start | bytes 4718600 | tf_op jit(solution)/shard_map/ppermute | solution.py:22
  769.4 52.1 %collective-permute-start.5 = (f32[2,8,768,48]{2,3,1,0:T(8,128)}, f32[2,8,768,48]{2,3,1,0:T(8,128)}, u32[]{:S(2)}, u32[]{:S(2)}) collective-permute-start(f32[2,8,768,48]{2,3,1,0:T(8,128)} %pad_maximum_fusion.2), channel_id=1, source_target_pairs={{0,4},{1,5},{2,6},{3,7},{4,0},{5,1},{6,2},{7,3},{8,12},{9,13},{10,... | collective-permute-start | bytes 7077896 | tf_op jit(solution)/shard_map/ppermute | solution.py:22
  827.3 100.3 %collective-permute-start.6 = (f32[2,8,896,48]{2,3,1,0:T(8,128)}, f32[2,8,896,48]{2,3,1,0:T(8,128)}, u32[]{:S(2)}, u32[]{:S(2)}) collective-permute-start(f32[2,8,896,48]{2,3,1,0:T(8,128)} %pad_maximum_fusion.1), channel_id=1, source_target_pairs={{0,2},{1,3},{2,0},{3,1},{4,6},{5,7},{6,4},{7,5},{8,10},{9,11},{10,... | collective-permute-start | bytes 8257544 | tf_op jit(solution)/shard_map/ppermute | solution.py:22
  935.1 166.5 %collective-permute-start.7 = (f32[2,8,960,48]{2,3,1,0:T(8,128)}, f32[2,8,960,48]{2,3,1,0:T(8,128)}, u32[]{:S(2)}, u32[]{:S(2)}) collective-permute-start(f32[2,8,960,48]{2,3,1,0:T(8,128)} %pad_maximum_fusion), channel_id=1, source_target_pairs={{0,1},{1,0},{2,3},{3,2},{4,5},{5,4},{6,7},{7,6},{8,9},{9,8},{10,11... | collective-permute-start | bytes 8847368 | tf_op jit(solution)/shard_map/ppermute | solution.py:22
  941.3 119.7 %copy-start.235 = (f32[64,8]{0,1:T(8,128)S(1)}, f32[64,8]{0,1:T(8,128)}, u32[]{:S(2)}) copy-start(f32[64,8]{0,1:T(8,128)} %copy-done.234) | copy-start | bytes 6148
  1199.7 417.7 %all-reduce.12.cloned.1.call-start = ((), (), s32[]{:S(2)}) async-start(), calls=%async_computation.2 | async-start | bytes 28311552 | tf_op jit(solution)/shard_map/psum | solution.py:403
  1252.3 97.8 %copy-start.6 = (bf16[1024,768]{1,0:T(8,128)(2,1)S(1)}, bf16[1024,768]{1,0:T(8,128)(2,1)}, u32[]{:S(2)}) copy-start(bf16[1024,768]{1,0:T(8,128)(2,1)} %param.35) | copy-start | bytes 4718596
  1252.3 97.8 %copy-start.166 = (f32[1024]{0:T(1024)S(1)}, f32[1024]{0:T(1024)}, u32[]{:S(2)}) copy-start(f32[1024]{0:T(1024)} %copy-done.165) | copy-start | bytes 12292
  1252.3 97.8 %copy-start.176 = (f32[768]{0:T(1024)S(1)}, f32[768]{0:T(1024)}, u32[]{:S(2)}) copy-start(f32[768]{0:T(1024)} %param.38) | copy-start | bytes 9220
  (237 other events, 1747.1 us)
Sparse Core Ops, SparseCore 0:
  390.6 84.9 all-reduce.7
  500.5 85.7 all-reduce.9
  1199.8 150.2 all-reduce.13
  1357.0 260.2 all-reduce.11
where the time goes:
time: 1660 us; the launch traced here: 1640 us
  local copies, waits for them, and re-layouts  481 us (29%)
  waiting for transfers between devices  439 us (26%)
  matrix products  412 us (25%)
  other arithmetic  212 us (13%)
  blocking collectives  60.4 us (4%)
  between operations  17.4 us (1%)
    broadcast_in_dim x90, local copies, waits for them, and re-layouts, spread_rows(): jnp.where(chosen_mask, moved[:, None], jnp.zeros((), values.dtype))  211 us
    psum x1, waiting for transfers between devices, local(): lax.psum((grad_ln1_gain, grad_ln1_shift, grad_w_query, grad_b_query, grad...  194 us
    psum x1, waiting for transfers between devices, local(): lax.psum(jnp.dot(hidden_low, w_down, preferred_element_type=jnp.float32),...  90.1 us
    psum x1, waiting for transfers between devices, local(): lax.psum(jnp.dot(merged_low, w_out, preferred_element_type=jnp.float32),...  84.6 us
    dot_general x45, matrix products, masked_scores(): jnp.einsum('uqd,ukd->uqk', queries, key_units, preferred_element_type=jnp...  73.4 us
    dot_general x23, matrix products, both_grads_block(): jnp.einsum('uqk,uqd->ukd', score_grad, queries, preferred_element_type=jn...  66.2 us
    reduce_sum x20, other arithmetic, pick_rows(): jnp.sum(jnp.where(chosen_mask, shaped, jnp.zeros((), values.dtype)), axis...  65.1 us
    dot_general x23, matrix products, both_grads_block(): jnp.einsum('uqk,ukd->uqd', score_grad, key_units, preferred_element_type=...  63.7 us
  transfers between devices with their start and end apart: 12, of which 6 were waited for; matrix products, arithmetic and copies ran while one was open for 45% of the time, Pallas kernels for 0%

commit v1 on v0

--- a/solution.py
+++ b/solution.py
@@ -1,9 +1,11 @@
-from functools import reduce
+from functools import partial, reduce
 import math
 
 import jax
 import jax.numpy as jnp
 from jax import lax
+from jax.experimental import pallas as pl
+from jax.experimental.pallas import tpu as pltpu
 from jax.sharding import PartitionSpec as P
 
 HEAD_DIM = 48
@@ -14,6 +16,14 @@
 EPSILON = 1e-05
 MASKED = -1000000000.0
 GELU_SCALE = 0.7978845608028654
+F32 = jnp.float32
+BF16 = jnp.bfloat16
+HEADS_HERE = 8
+QKV = 3 * HEAD_DIM
+AUG = 16
+OUT_ROWS = HEAD_DIM + AUG
+NT = (((1,), (1,)), ((), ()))
+TN = (((0,), (0,)), ((), ()))
 
 
 def partner(value, axis, bit):
@@ -151,7 +161,7 @@
     return blocks
 
 
-def local(
+def local_general(
     tokens,
     doc_ids,
     valid,
@@ -441,6 +451,707 @@
     )
 
 
+def bitrev(value, bits):
+    return sum((value >> at & 1) << (bits - 1 - at) for at in range(bits))
+
+
+def class_lanes(head, branch):
+    size = SEG0 >> branch
+    start = bitrev(head % 2**branch, branch) * size
+    return slice(start, start + size)
+
+
+LANES0 = {1: (0, 512), 2: (512, 256), 3: (768, 128), 4: (896, 64)}
+LANES1 = {2: (0, 512), 3: (512, 256), 4: (768, 128)}
+LANES2 = {3: (0, 512), 4: (512, 256)}
+
+
+def one_hot_rows(forward):
+    row = lax.broadcasted_iota(jnp.int32, (SEG0, SEG0), 0)
+    col = lax.broadcasted_iota(jnp.int32, (SEG0, SEG0), 1)
+    place, slot = (row, col) if forward else (col, row)
+    group = place // 64
+    rev = (group & 1) * 8 + (group >> 1 & 1) * 4 + (group >> 2 & 1) * 2 + (group >> 3 & 1)
+    return jnp.where(rev + 16 * (place % 64) == slot, 1.0, 0.0).astype(BF16)
+
+
+def split_three(value):
+    high = value.astype(BF16).astype(F32)
+    rest = value - high
+    mid = rest.astype(BF16).astype(F32)
+    return high, mid, rest - mid
+
+
+def rows_iota(count, lanes):
+    return lax.broadcasted_iota(jnp.int32, (count, lanes), 0)
+
+
+def project_kernel(
+    pos_ref, tok_ref, gain_ref, shift_ref, wq_ref, bq_ref, wk_ref, wv_ref, bv_ref, all_ref, send_ref, normed_ref
+):
+    dl = pos_ref[0]
+    unit = pos_ref[1]
+    values = tok_ref[...].astype(F32)
+    centred = values - jnp.mean(values, axis=-1, keepdims=True)
+    row_var = jnp.mean(centred * centred, axis=-1, keepdims=True)
+    normed = (centred * lax.rsqrt(row_var + EPSILON) * gain_ref[...] + shift_ref[...]).astype(BF16)
+    order = one_hot_rows(False)
+    normed_t = lax.dot_general(normed, order, TN, preferred_element_type=F32).astype(BF16)
+    normed_ref[...] = normed_t
+
+    def project(w_ref):
+        return lax.dot_general(w_ref[...], normed_t, TN, preferred_element_type=F32)
+
+    query = ((project(wq_ref) + bq_ref[...]) * HEAD_DIM**-0.5).astype(BF16)
+    key = project(wk_ref).astype(BF16)
+    value = (project(wv_ref) + bv_ref[...]).astype(BF16)
+    for head in range(HEADS_HERE):
+        own = slice(head * HEAD_DIM, (head + 1) * HEAD_DIM)
+        for at, part in enumerate((query, key, value)):
+            rows = slice(at * HEAD_DIM, (at + 1) * HEAD_DIM)
+            here = part[own]
+            all_ref[head, rows, :] = here
+            for branch in (1, 2, 3):
+                start, size = LANES0[branch]
+                send_ref[head ^ dl, rows, start : start + size] = here[:, class_lanes(head, branch)]
+            both = here[:, class_lanes(head, 3)]
+            picked = jnp.where(unit == 0, both[:, :64].astype(F32), both[:, 64:].astype(F32))
+            send_ref[head ^ dl, rows, 896:960] = picked.astype(BF16)
+            send_ref[head ^ dl, rows, 960:1024] = jnp.zeros((HEAD_DIM, 64), BF16)
+
+
+def whole_spec(shape):
+    return pl.BlockSpec(shape, lambda *_: (0,) * len(shape))
+
+
+def project_call(place, tokens, gain, shift, w_query, b_query, w_key, w_value, b_value):
+    width = HEADS_HERE * HEAD_DIM
+    model = tokens.shape[1]
+    args = (tokens, gain[None], shift[None], w_query, b_query[:, None], w_key, w_value, b_value[:, None])
+    out_shape = [
+        jax.ShapeDtypeStruct((HEADS_HERE, QKV, SEG0), BF16),
+        jax.ShapeDtypeStruct((HEADS_HERE, QKV, SEG0), BF16),
+        jax.ShapeDtypeStruct((model, SEG0), BF16),
+    ]
+    return pl.pallas_call(
+        project_kernel,
+        grid_spec=pltpu.PrefetchScalarGridSpec(
+            num_scalar_prefetch=1,
+            grid=(1,),
+            in_specs=[whole_spec(a.shape) for a in args],
+            out_specs=[whole_spec(o.shape) for o in out_shape],
+        ),
+        out_shape=out_shape,
+        name="project",
+        cost_estimate=pl.CostEstimate(
+            flops=2 * SEG0 * model * (3 * width + SEG0), bytes_accessed=12 * 2**20, transcendentals=SEG0
+        ),
+    )(place, *args)
+
+
+def key_tail(tags):
+    at = rows_iota(AUG, tags.shape[1])
+    return jnp.where((at == tags) | (at > 12), 1.0, 0.0).astype(BF16)
+
+
+def query_tail(tags):
+    at = rows_iota(AUG, tags.shape[1])
+    return jnp.where((at == tags) | (at > 12), 0.0, MASKED)
+
+
+def gather_rows(pieces, rows):
+    return jnp.concatenate([ref[0, rows[0] : rows[1], :size] for ref, size in pieces], axis=1)
+
+
+def forward_kernel(*refs, sizes, tile, packed):
+    count = len(sizes)
+    piece_refs, (tag_ref,) = refs[:count], refs[count : count + 1]
+    outs = refs[count + 1 :]
+    shared = count if len(sizes) < 5 else count - 1
+    q_pieces = [(piece_refs[i], sizes[i]) for i in range(shared)]
+    kv_pieces = q_pieces
+    query = gather_rows(q_pieces, (0, HEAD_DIM))
+    key = gather_rows(kv_pieces, (HEAD_DIM, 2 * HEAD_DIM))
+    value = gather_rows(kv_pieces, (2 * HEAD_DIM, QKV))
+    if shared < count:
+        last = piece_refs[-1]
+        key = jnp.concatenate([key, last[0, :HEAD_DIM, :]], axis=1)
+        value = jnp.concatenate([value, last[0, HEAD_DIM : 2 * HEAD_DIM, :]], axis=1)
+    tags = tag_ref[0]
+    keys = key.shape[1]
+    key_rows = jnp.concatenate([key, key_tail(tags)], axis=0).T
+    ones = jnp.where(rows_iota(AUG, keys) == 0, 1.0, 0.0).astype(BF16)
+    value_aug = jnp.concatenate([value, ones], axis=0)
+    query_aug = jnp.concatenate([query, query_tail(tags[:, : query.shape[1]]).astype(BF16)], axis=0)
+    for start in range(0, query.shape[1], tile):
+        lanes = slice(start, start + tile)
+        scores = jnp.dot(key_rows, query_aug[:, lanes], preferred_element_type=F32)
+        peak = jnp.max(scores, axis=0, keepdims=True)
+        weights = jnp.exp(scores - peak).astype(BF16)
+        summed = jnp.dot(value_aug, weights, preferred_element_type=F32)
+        total = summed[HEAD_DIM : HEAD_DIM + 1]
+        outputs = summed[:HEAD_DIM] / total
+        lse = peak + jnp.log(total)
+        if packed:
+            (o_ref,) = outs
+            o_ref[0, :HEAD_DIM, lanes] = outputs.astype(BF16)
+            high, mid, low = split_three(lse)
+            at = rows_iota(AUG, tile)
+            tail = jnp.where(at == 0, high, jnp.where(at == 1, mid, jnp.where(at == 2, low, 0.0)))
+            o_ref[0, HEAD_DIM:, lanes] = tail.astype(BF16)
+        else:
+            o_ref, lse_ref = outs
+            o_ref[0, :, lanes] = outputs
+            lse_ref[0, :, lanes] = lse
+
+
+def backward_kernel(*refs, sizes, grad_sizes, tile, out_type):
+    count, grads = len(sizes), len(grad_sizes)
+    piece_refs = refs[:count]
+    grad_refs = refs[count : count + grads]
+    tag_ref, out_ref = refs[count + grads : count + grads + 2]
+    kv_out_ref = refs[-1]
+    shared = count if count < 5 else count - 1
+    pieces = [(piece_refs[i], sizes[i]) for i in range(shared)]
+    query = gather_rows(pieces, (0, HEAD_DIM))
+    key = gather_rows(pieces, (HEAD_DIM, 2 * HEAD_DIM))
+    value = gather_rows(pieces, (2 * HEAD_DIM, QKV))
+    if shared < count:
+        last = piece_refs[-1]
+        key = jnp.concatenate([key, last[0, :HEAD_DIM, :]], axis=1)
+        value = jnp.concatenate([value, last[0, HEAD_DIM : 2 * HEAD_DIM, :]], axis=1)
+    grad_pieces = [(grad_refs[i], grad_sizes[i]) for i in range(grads)]
+    grad = gather_rows(grad_pieces, (0, HEAD_DIM))
+    tail = gather_rows(grad_pieces, (HEAD_DIM, OUT_ROWS)).astype(F32)
+    tags = tag_ref[0]
+    keys, queries = key.shape[1], query.shape[1]
+    key_rows = jnp.concatenate([key, key_tail(tags)], axis=0).T
+    ones = jnp.where(rows_iota(AUG, keys) < 3, 1.0, 0.0).astype(BF16)
+    value_rows = jnp.concatenate([value, ones], axis=0).T
+    at = rows_iota(AUG, queries)
+    mask = query_tail(tags[:, :queries])
+    query_aug = jnp.concatenate([query, jnp.where(at > 12, tail, mask).astype(BF16)], axis=0)
+    grad_aug = jnp.concatenate([grad, jnp.where(at < 3, tail, 0.0).astype(BF16)], axis=0)
+    key_grad = jnp.zeros((HEAD_DIM, keys), F32)
+    value_grad = jnp.zeros((HEAD_DIM, keys), F32)
+    for start in range(0, queries, tile):
+        lanes = slice(start, start + tile)
+        probs = jnp.exp(jnp.dot(key_rows, query_aug[:, lanes], preferred_element_type=F32))
+        prob_grad = jnp.dot(value_rows, grad_aug[:, lanes], preferred_element_type=F32)
+        score_grad = (probs * prob_grad).astype(BF16)
+        probs_low = probs.astype(BF16)
+        out_ref[0, :HEAD_DIM, lanes] = jnp.dot(key, score_grad, preferred_element_type=F32).astype(out_type)
+        key_grad = key_grad + lax.dot_general(query[:, lanes], score_grad, NT, preferred_element_type=F32)
+        value_grad = value_grad + lax.dot_general(grad[:, lanes], probs_low, NT, preferred_element_type=F32)
+    if shared < count:
+        half = keys // 2
+        out_ref[0, HEAD_DIM : 2 * HEAD_DIM, :] = key_grad[:, :half].astype(out_type)
+        out_ref[0, 2 * HEAD_DIM :, :] = value_grad[:, :half].astype(out_type)
+        kv_out_ref[0, :HEAD_DIM, :] = key_grad[:, half:].astype(out_type)
+        kv_out_ref[0, HEAD_DIM:, :] = value_grad[:, half:].astype(out_type)
+    else:
+        out_ref[0, HEAD_DIM : 2 * HEAD_DIM, :] = key_grad.astype(out_type)
+        out_ref[0, 2 * HEAD_DIM :, :] = value_grad.astype(out_type)
+
+
+def lane_spec(rows, start, size):
+    block = max(size, 128)
+    return pl.BlockSpec((1, rows, block), lambda head, at=start // block: (head, 0, at))
+
+
+def branch_pieces(branch, parts):
+    if branch == 0:
+        return [(parts[0], 0, SEG0)]
+    pieces = [(parts[0],) + LANES0[branch], (parts[1],) + LANES0[branch]]
+    if branch > 1:
+        pieces.append((parts[2],) + LANES1[branch])
+    if branch > 2:
+        pieces.append((parts[3],) + LANES2[branch])
+    return pieces
+
+
+def forward_call(branch, parts, tags):
+    pieces = branch_pieces(branch, parts)
+    queries = sum(piece[2] for piece in pieces)
+    if branch == 4:
+        pieces.append((parts[4], 0, 512))
+    heads = 8 >> min(branch, 3)
+    packed = branch > 0
+    if packed:
+        out_shape = [jax.ShapeDtypeStruct((heads, OUT_ROWS, queries), BF16)]
+        out_specs = [pl.BlockSpec((1, OUT_ROWS, queries), lambda head: (head, 0, 0))]
+    else:
+        out_shape = [
+            jax.ShapeDtypeStruct((heads, HEAD_DIM, queries), F32),
+            jax.ShapeDtypeStruct((heads, 1, queries), F32),
+        ]
+        out_specs = [
+            pl.BlockSpec((1, HEAD_DIM, queries), lambda head: (head, 0, 0)),
+            pl.BlockSpec((1, 1, queries), lambda head: (head, 0, 0)),
+        ]
+    return pl.pallas_call(
+        partial(forward_kernel, sizes=tuple(piece[2] for piece in pieces), tile=512, packed=packed),
+        grid=(heads,),
+        in_specs=[lane_spec(array.shape[1], start, size) for array, start, size in pieces]
+        + [pl.BlockSpec((1, 1, SEG0), lambda head: (head, 0, 0))],
+        out_specs=out_specs,
+        out_shape=out_shape,
+        name=f"attend{branch}",
+        cost_estimate=pl.CostEstimate(
+            flops=heads * queries * SEG0 * 2 * 512, bytes_accessed=heads * SEG0 * 512, transcendentals=heads * queries * SEG0
+        ),
+    )(*[piece[0] for piece in pieces], tags)
+
+
+def backward_call(branch, parts, grad_parts, tags):
+    pieces = branch_pieces(branch, parts)
+    grad_pieces = branch_pieces(branch, grad_parts)
+    queries = sum(piece[2] for piece in pieces)
+    heads = 8 >> min(branch, 3)
+    out_type = F32 if branch == 0 else BF16
+    out_shape = [jax.ShapeDtypeStruct((heads, QKV, queries), out_type)]
+    if branch == 4:
+        pieces.append((parts[4], 0, 512))
+        out_shape.append(jax.ShapeDtypeStruct((heads, 2 * HEAD_DIM, 512), out_type))
+    return pl.pallas_call(
+        partial(
+            backward_kernel,
+            sizes=tuple(piece[2] for piece in pieces),
+            grad_sizes=tuple(piece[2] for piece in grad_pieces),
+            tile=512,
+            out_type=out_type,
+        ),
+        grid=(heads,),
+        in_specs=[lane_spec(array.shape[1], start, size) for array, start, size in pieces + grad_pieces]
+        + [pl.BlockSpec((1, 1, SEG0), lambda head: (head, 0, 0))],
+        out_specs=[pl.BlockSpec((1,) + out.shape[1:], lambda head: (head, 0, 0)) for out in out_shape],
+        out_shape=out_shape,
+        name=f"attend_back{branch}",
+        cost_estimate=pl.CostEstimate(
+            flops=heads * queries * SEG0 * 2 * 768, bytes_accessed=heads * SEG0 * 1024, transcendentals=heads * queries * SEG0
+        ),
+    )(*[piece[0] for piece in pieces + grad_pieces], tags)
+
+
+def branch_blocks(head, unit, ref, rows, at):
+    blocks = []
+    for branch in (1, 2, 3):
+        start, size = LANES0[branch]
+        blocks.append((class_lanes(head, branch), ref[at, rows[0] : rows[1], start : start + size].astype(F32)))
+    last = ref[at, rows[0] : rows[1], 896:960].astype(F32)
+    twice = jnp.concatenate([last, last], axis=1)
+    lane = lax.broadcasted_iota(jnp.int32, twice.shape, 1)
+    blocks.append((class_lanes(head, 3), twice, (lane >= 64) == (unit == 1)))
+    return blocks
+
+
+def merge_kernel(pos_ref, o_ref, lse_ref, back_ref, merged_ref, total_ref):
+    dl = pos_ref[0]
+    unit = pos_ref[1]
+    for head in range(HEADS_HERE):
+        at = head ^ dl
+        peak = lse_ref[head]
+        tails = branch_blocks(head, unit, back_ref, (HEAD_DIM, OUT_ROWS), at)
+        lses = []
+        for block in tails:
+            value = block[1][0:1] + block[1][1:2] + block[1][2:3]
+            if len(block) == 3:
+                value = jnp.where(block[2][0:1], value, MASKED)
+            lses.append((block[0], value))
+        full = [lse_ref[head]]
+        for lanes, value in lses:
+            pad = []
+            if lanes.start:
+                pad.append(jnp.full((1, lanes.start), MASKED, F32))
+            pad.append(value)
+            if lanes.stop < SEG0:
+                pad.append(jnp.full((1, SEG0 - lanes.stop), MASKED, F32))
+            full.append(jnp.concatenate(pad, axis=1))
+        peak = reduce(jnp.maximum, full)
+        weights = [jnp.exp(value - peak) for value in full]
+        summed = reduce(jnp.add, weights)
+        total_ref[head] = peak + jnp.log(summed)
+        shares = [weight / summed for weight in weights]
+        rows = slice(head * HEAD_DIM, (head + 1) * HEAD_DIM)
+        merged_ref[rows, :] = o_ref[head] * shares[0]
+        outs = branch_blocks(head, unit, back_ref, (0, HEAD_DIM), at)
+        for block, share in zip(outs, shares[1:]):
+            merged_ref[rows, block[0]] += block[1] * share[:, block[0]]
+
+
+def merge_call(place, outputs, lse, back):
+    width = HEADS_HERE * HEAD_DIM
+    out_shape = [jax.ShapeDtypeStruct((width, SEG0), F32), jax.ShapeDtypeStruct((HEADS_HERE, 1, SEG0), F32)]
+    args = (outputs, lse, back)
+    return pl.pallas_call(
+        merge_kernel,
+        grid_spec=pltpu.PrefetchScalarGridSpec(
+            num_scalar_prefetch=1,
+            grid=(1,),
+            in_specs=[whole_spec(a.shape) for a in args],
+            out_specs=[whole_spec(o.shape) for o in out_shape],
+        ),
+        out_shape=out_shape,
+        name="merge",
+        cost_estimate=pl.CostEstimate(flops=10**8, bytes_accessed=6 * 2**20, transcendentals=SEG0 * 8),
+    )(place, *args)
+
+
+def spread_kernel(pos_ref, grad_ref, merged_ref, total_ref, all_ref, send_ref):
+    dl = pos_ref[0]
+    unit = pos_ref[1]
+    at = rows_iota(AUG, SEG0)
+    for head in range(HEADS_HERE):
+        rows = slice(head * HEAD_DIM, (head + 1) * HEAD_DIM)
+        grad = grad_ref[rows, :]
+        delta = jnp.sum(grad.astype(F32) * merged_ref[rows, :], axis=0, keepdims=True)
+        parts = split_three(-delta) + split_three(-total_ref[head])
+        tail = jnp.zeros((AUG, SEG0), F32)
+        for row, part in zip((0, 1, 2, 13, 14, 15), parts):
+            tail = jnp.where(at == row, part, tail)
+        for place, here in ((slice(0, HEAD_DIM), grad), (slice(HEAD_DIM, OUT_ROWS), tail.astype(BF16))):
+            all_ref[head, place, :] = here
+            for branch in (1, 2, 3):
+                start, size = LANES0[branch]
+                send_ref[head ^ dl, place, start : start + size] = here[:, class_lanes(head, branch)]
+            both = here[:, class_lanes(head, 3)]
+            picked = jnp.where(unit == 0, both[:, :64].astype(F32), both[:, 64:].astype(F32))
+            send_ref[head ^ dl, place, 896:960] = picked.astype(BF16)
+            send_ref[head ^ dl, place, 960:1024] = jnp.zeros((here.shape[0], 64), BF16)
+
+
+def spread_call(place, grad, merged, total):
+    out_shape = [jax.ShapeDtypeStruct((HEADS_HERE, OUT_ROWS, SEG0), BF16)] * 2
+    args = (grad, merged, total)
+    return pl.pallas_call(
+        spread_kernel,
+        grid_spec=pltpu.PrefetchScalarGridSpec(
+            num_scalar_prefetch=1,
+            grid=(1,),
+            in_specs=[whole_spec(a.shape) for a in args],
+            out_specs=[whole_spec(o.shape) for o in out_shape],
+        ),
+        out_shape=out_shape,
+        name="spread",
+        cost_estimate=pl.CostEstimate(flops=10**8, bytes_accessed=5 * 2**20, transcendentals=0),
+    )(place, *args)
+
+
+def collect_kernel(pos_ref, own_ref, back_ref, out_ref, sum_ref):
+    dl = pos_ref[0]
+    unit = pos_ref[1]
+    width = HEADS_HERE * HEAD_DIM
+    for head in range(HEADS_HERE):
+        sum_ref[...] = own_ref[head]
+        for block in branch_blocks(head, unit, back_ref, (0, QKV), head ^ dl):
+            value = block[1] if len(block) == 2 else jnp.where(block[2], block[1], 0.0)
+            sum_ref[:, block[0]] += value
+        for at in range(3):
+            out_ref[at * width + head * HEAD_DIM : at * width + (head + 1) * HEAD_DIM, :] = sum_ref[
+                at * HEAD_DIM : (at + 1) * HEAD_DIM, :
+            ].astype(BF16)
+
+
+def collect_call(place, own, back):
+    out_shape = jax.ShapeDtypeStruct((HEADS_HERE * QKV, SEG0), BF16)
+    args = (own, back)
+    return pl.pallas_call(
+        collect_kernel,
+        grid_spec=pltpu.PrefetchScalarGridSpec(
+            num_scalar_prefetch=1,
+            grid=(1,),
+            in_specs=[whole_spec(a.shape) for a in args],
+            out_specs=whole_spec(out_shape.shape),
+            scratch_shapes=[pltpu.VMEM((QKV, SEG0), F32)],
+        ),
+        out_shape=out_shape,
+        name="collect",
+        cost_estimate=pl.CostEstimate(flops=10**8, bytes_accessed=9 * 2**20, transcendentals=0),
+    )(place, *args)
+
+
+def swap_unit(value):
+    return lax.ppermute(value, "unit", [(0, 1), (1, 0)])
+
+
+def cat(*parts):
+    return jnp.concatenate(parts, axis=2)
+
+
+def step1_rows(own, first):
+    return cat(
+        *[array[2:4, :, start : start + size] for start, size in (LANES0[2], LANES0[3], LANES0[4]) for array in (own, first)]
+    )
+
+
+def step2_rows(own, first, second):
+    pieces = []
+    for branch in (3, 4):
+        for array in (own, first):
+            start, size = LANES0[branch]
+            pieces.append(array[1:2, :, start : start + size])
+        start, size = LANES1[branch]
+        pieces.append(second[1:2, :, start : start + size])
+    return cat(*pieces)
+
+
+def step3_rows(own, first, second, third):
+    rows = slice(HEAD_DIM, QKV)
+    return cat(
+        own[0:1, rows, 896:960], first[0:1, rows, 896:960], second[0:1, rows, 768:896], third[0:1, rows, 512:768]
+    )
+
+
+def send_down(own, copy_last):
+    first = partner(own[4:8, :, :960], "row", 0)
+    second = partner(step1_rows(own, first), "row", 1)
+    third = partner(step2_rows(own, first, second), "row", 2)
+    parts = [own, first, second, third]
+    if copy_last:
+        parts.append(partner(step3_rows(*parts), "row", 3))
+    return parts
+
+
+def send_up(out1, out2, out3, out4):
+    third = partner(cat(out3[:, :, 512:1024], out4[:, :, 256:512]), "row", 2)
+
+    def joined(low, high):
+        return jnp.concatenate([low, high], axis=0)
+
+    second = partner(
+        cat(
+            out2[:, :, 512:1024],
+            joined(out3[:, :, 256:512], third[:, :, 256:512]),
+            joined(out4[:, :, 128:256], third[:, :, 640:768]),
+        ),
+        "row",
+        1,
+    )
+
+    def rows_of(at):
+        return cat(
+            out1[:, :, 512 * at : 512 * at + 512],
+            joined(out2[:, :, 256 * at : 256 * at + 256], second[:, :, 256 * at : 256 * at + 256]),
+            jnp.concatenate(
+                [
+                    out3[:, :, 128 * at : 128 * at + 128],
+                    third[:, :, 128 * at : 128 * at + 128],
+                    second[:, :, 512 + 128 * at : 640 + 128 * at],
+                ],
+                axis=0,
+            ),
+            jnp.concatenate(
+                [
+                    out4[:, :, 64 * at : 64 * at + 64],
+                    third[:, :, 512 + 64 * at : 576 + 64 * at],
+                    second[:, :, 768 + 64 * at : 832 + 64 * at],
+                ],
+                axis=0,
+            ),
+        )
+
+    first = partner(rows_of(1), "row", 0)
+    return joined(rows_of(0), first)
+
+
+def sum_rows(value):
+    place = lax.axis_index("row")
+    for bit in range(4):
+        half = value.shape[0] // 2
+        upper = place >> bit & 1
+        kept = lax.dynamic_slice_in_dim(value, upper * half, half)
+        sent = lax.dynamic_slice_in_dim(value, (1 - upper) * half, half)
+        value = (kept.astype(F32) + partner(sent, "row", bit).astype(F32)).astype(BF16)
+    for bit in reversed(range(4)):
+        upper = place >> bit & 1 == 1
+        theirs = partner(value, "row", bit)
+        value = jnp.where(
+            upper, jnp.concatenate([theirs, value], axis=0), jnp.concatenate([value, theirs], axis=0)
+        )
+    return value
+
+
+def sum_small(value):
+    for bit in range(4):
+        value = value + partner(value, "row", bit)
+    return value
+
+
+def branch_tags(doc_ids, valid, place, unit):
+    tags = jnp.where(valid == 1, doc_ids + 1, 0).reshape(16, 64, 2, 2, 2, 2)
+    tags = tags.transpose(0, 5, 4, 3, 2, 1).reshape(16, SEG0)
+    tags = jnp.take(tags, jnp.arange(16, dtype=jnp.int32) ^ place, axis=0)
+    bit0, bit1, bit2 = place & 1, place >> 1 & 1, place >> 2 & 1
+    dl = 4 * bit0 + 2 * bit1 + bit2
+    result = [jnp.broadcast_to(tags[0][None, None], (8, 1, SEG0))]
+    for branch in range(1, 5):
+        rows = []
+        size = SEG0 >> branch
+        for relative in range(8 >> min(branch, 3)):
+            group = (8 * unit + (relative ^ dl)) % 2**branch
+            start = bitrev(group, branch) * size
+            rows.append(lax.dynamic_slice(tags[: 2**branch], (0, start), (2**branch, size)).reshape(1, SEG0))
+        result.append(jnp.stack(rows))
+    return result, dl
+
+
+def local(
+    tokens,
+    doc_ids,
+    valid,
+    ln1_gain,
+    ln1_shift,
+    w_query,
+    b_query,
+    w_key,
+    w_value,
+    b_value,
+    w_out,
+    b_out,
+    ln2_gain,
+    ln2_shift,
+    w_up,
+    b_up,
+    w_down,
+    b_down,
+    cotangent,
+):
+    width = HEADS_HERE * HEAD_DIM
+    scaling = HEAD_DIM**-0.5
+    unit = lax.axis_index("unit")
+    row = lax.axis_index("row")
+    tags, dl = branch_tags(doc_ids, valid, row, unit)
+    place = jnp.stack([dl, unit]).astype(jnp.int32)
+
+    everything, sent, normed_t = project_call(
+        place, tokens, ln1_gain, ln1_shift, w_query, b_query, w_key, w_value, b_value
+    )
+    parts = send_down(sent, True)
+    out0, lse0 = forward_call(0, [everything], tags[0])
+    outs = [forward_call(branch, parts, tags[branch])[0] for branch in range(1, 5)]
+    back = send_up(*outs)
+    merged_t, total = merge_call(place, out0, lse0, back)
+    merged_low = merged_t.astype(BF16)
+
+    order = one_hot_rows(True)
+    residual = jnp.dot(order, tokens, preferred_element_type=F32)
+    cot = jnp.dot(order, cotangent, preferred_element_type=F32).astype(BF16)
+
+    def both_units(part):
+        low = part.astype(BF16)
+        return low.astype(F32) + swap_unit(low).astype(F32)
+
+    attention = both_units(lax.dot_general(merged_low, w_out, TN, preferred_element_type=F32)) + b_out
+    middle = residual + attention
+    normed2 = layer_norm(middle, ln2_gain, ln2_shift)
+    normed2_low = normed2.astype(BF16)
+    up_input = jnp.dot(normed2_low, w_up, preferred_element_type=F32) + b_up
+    hidden_low = gelu_tanh(up_input).astype(BF16)
+    back_rows = cot.astype(F32)
+    hidden_grad = lax.dot_general(cot, w_down, NT, preferred_element_type=F32)
+    _, gelu_pull = jax.vjp(gelu_tanh, up_input)
+    up_grad = gelu_pull(hidden_grad)[0].astype(BF16)
+    normed2_grad = both_units(lax.dot_general(up_grad, w_up, NT, preferred_element_type=F32))
+    feed_out = both_units(jnp.dot(hidden_low, w_down, preferred_element_type=F32)) + b_down
+    mixed_out = (middle + feed_out).astype(BF16)
+    grad_b_down = jnp.sum(back_rows, axis=0)
+    grad_w_down = lax.dot_general(hidden_low, cot, TN, preferred_element_type=F32)
+    grad_b_up = jnp.sum(up_grad.astype(F32), axis=0)
+    grad_w_up = lax.dot_general(normed2_low, up_grad, TN, preferred_element_type=F32)
+    _, norm2_pull = jax.vjp(layer_norm, middle, ln2_gain, ln2_shift)
+    middle_part, grad_ln2_gain, grad_ln2_shift = norm2_pull(normed2_grad)
+    middle_grad = back_rows + middle_part
+    attention_grad = middle_grad.astype(BF16)
+    grad_b_out = jnp.sum(attention_grad.astype(F32), axis=0)
+    grad_w_out = jnp.dot(merged_low, attention_grad, preferred_element_type=F32)
+    merged_grad = lax.dot_general(w_out, attention_grad, NT, preferred_element_type=F32).astype(BF16)
+
+    grad_w_up, grad_w_down, grad_w_out = lax.psum(
+        (grad_w_up.astype(BF16), grad_w_down.astype(BF16), grad_w_out.astype(BF16)), "row"
+    )
+
+    grads_all, grads_sent = spread_call(place, merged_grad, merged_t, total)
+    grad_parts = send_down(grads_sent, False)
+    own_grads = backward_call(0, [everything], [grads_all], tags[0])[0]
+    back1, back2, back3 = [backward_call(b, parts, grad_parts, tags[b])[0] for b in (1, 2, 3)]
+    back4, back4_kv = backward_call(4, parts, grad_parts, tags[4])
+    other_kv = partner(back4_kv, "row", 3)
+    back4 = jnp.concatenate(
+        [back4[:, :HEAD_DIM], (back4[:, HEAD_DIM:].astype(F32) + other_kv.astype(F32)).astype(BF16)], axis=1
+    )
+    grads_back = send_up(back1, back2, back3, back4)
+    qkv_grad = collect_call(place, own_grads, grads_back)
+    query_grad, key_grad, value_grad = (qkv_grad[at * width : (at + 1) * width] for at in range(3))
+
+    grad_w_qkv = lax.dot_general(normed_t, qkv_grad, NT, preferred_element_type=F32)
+    grad_b_query = scaling * jnp.sum(query_grad.astype(F32), axis=1)
+    grad_b_value = jnp.sum(value_grad.astype(F32), axis=1)
+    normed_part = (
+        scaling * lax.dot_general(query_grad, w_query, (((0,), (1,)), ((), ())), preferred_element_type=F32)
+        + lax.dot_general(key_grad, w_key, (((0,), (1,)), ((), ())), preferred_element_type=F32)
+        + lax.dot_general(value_grad, w_value, (((0,), (1,)), ((), ())), preferred_element_type=F32)
+    )
+    normed_grad = both_units(normed_part)
+    _, norm1_pull = jax.vjp(layer_norm, residual, ln1_gain, ln1_shift)
+    input_part, grad_ln1_gain, grad_ln1_shift = norm1_pull(normed_grad)
+    grad_tokens = middle_grad + input_part
+
+    summed_qkv = sum_rows(grad_w_qkv.astype(BF16)).astype(F32)
+    grad_w_query, grad_w_key, grad_w_value = (summed_qkv[:, at * width : (at + 1) * width] for at in range(3))
+    vectors = (
+        grad_ln1_gain,
+        grad_ln1_shift,
+        grad_b_query,
+        grad_b_value,
+        grad_b_out,
+        grad_ln2_gain,
+        grad_ln2_shift,
+        grad_b_up,
+        grad_b_down,
+    )
+    lengths = [vector.shape[0] for vector in vectors]
+    flat = sum_small(jnp.concatenate(vectors).reshape(-1, 128)).reshape(-1)
+    ends = [sum(lengths[: at + 1]) for at in range(len(lengths))]
+    (
+        grad_ln1_gain,
+        grad_ln1_shift,
+        grad_b_query,
+        grad_b_value,
+        grad_b_out,
+        grad_ln2_gain,
+        grad_ln2_shift,
+        grad_b_up,
+        grad_b_down,
+    ) = (flat[end - length : end] for end, length in zip(ends, lengths))
+
+    disorder = one_hot_rows(False)
+    mixed_out = jnp.dot(disorder, mixed_out, preferred_element_type=F32).astype(BF16)
+    high = grad_tokens.astype(BF16)
+    low = (grad_tokens - high.astype(F32)).astype(BF16)
+    grad_tokens = jnp.dot(disorder, high, preferred_element_type=F32) + jnp.dot(
+        disorder, low, preferred_element_type=F32
+    )
+    return (
+        mixed_out,
+        grad_tokens,
+        grad_ln1_gain,
+        grad_ln1_shift,
+        grad_w_query * scaling,
+        grad_b_query,
+        grad_w_key,
+        grad_w_value,
+        grad_b_value,
+        grad_w_out.astype(F32),
+        grad_b_out,
+        grad_ln2_gain,
+        grad_ln2_shift,
+        grad_w_up.astype(F32),
+        grad_b_up,
+        grad_w_down.astype(F32),
+        grad_b_down,
+    )
+
+
 def solution(mesh):
     placed = (
         P("row", None),
@@ -463,8 +1174,10 @@
         P(),
         P("row", None),
     )
+    rows = dict(mesh.shape)["row"]
+    fast = rows == 16 and dict(mesh.shape)["unit"] == 2
     return jax.shard_map(
-        local,
+        local if fast else local_general,
         mesh=mesh,
         in_specs=placed,
         out_specs=(

time: 1660 us -> 569 us (0.34); the launches traced: 1640 us -> 562 us
  local copies, waits for them, and re-layouts: 481 us -> 85.5 us
  matrix products: 412 us -> 68.3 us
  waiting for transfers between devices: 439 us -> 204 us
  other arithmetic: 212 us -> 36.9 us
  Pallas kernels: 0 us -> 117 us
  blocking collectives: 60.4 us -> 0 us
  starting transfers between devices: 13.7 us -> 35.3 us
    dot_general x178 -> x18, matrix products: 412 us -> 68.3 us  [the longest x1 9.26 us: local(): hidden_grad = lax.dot_general(cot, w_down, NT, preferred_element_type=F32)]
    psum x4 -> x1, waiting for transfers between devices: 388 us -> 99.6 us  [local(): lax.psum((grad_w_up.astype(BF16), grad_w_down.astype(BF16), grad_w_out.as...]
    broadcast_in_dim x102 -> x5, local copies, waits for them, and re-layouts: 216 us -> 6.25 us  [the longest x1 1.47 us: project_call(): b_query[:, None]]
    pallas_call x0 -> x14, Pallas kernels: none -> 117 us  [the longest x5 52.8 us: backward_call(): pl.pallas_call(partial(backward_kernel, sizes=tuple((piece[2] for piece i...]
    reduce_sum x47 -> x2, other arithmetic: 95.3 us -> 1.85 us  [the longest x1 1.58 us: local(): grad_b_out = jnp.sum(attention_grad.astype(F32), axis=0)]
    psum x1 -> x0, blocking collectives: 60.4 us -> none  [local(): lax.psum((grad_ln1_gain, grad_ln1_shift, grad_w_query, grad_b_query, grad...]
    ppermute x0 -> x4, waiting for transfers between devices: none -> 49.5 us  [swap_unit(): return lax.ppermute(value, 'unit', [(0, 1), (1, 0)])]
    another operation x28 -> x9, local copies, waits for them, and re-layouts: 53.2 us -> 4.62 us  [branch_tags(): result.append(jnp.stack(rows))]
  transfers between devices with their start and end apart: 12 -> 31, of which waited for: 6 -> 14; matrix products, arithmetic and copies ran while one was open for 45% -> 25% of each run, Pallas kernels for 0% -> 18%
where the time goes in v1:
time: 569 us; the launch traced here: 562 us
  waiting for transfers between devices  204 us (36%)
  Pallas kernels  117 us (21%)
  local copies, waits for them, and re-layouts  85.5 us (15%)
  matrix products  68.3 us (12%)
  other arithmetic  36.9 us (6%)
  starting transfers between devices  35.3 us (6%)
  between operations  15.5 us (3%)
    psum x1, waiting for transfers between devices, local(): lax.psum((grad_w_up.astype(BF16), grad_w_down.astype(BF16), grad_w_out.as...  99.6 us
    ppermute x26, waiting for transfers between devices, partner(): return lax.ppermute(value, axis, pairs)  55.2 us
    pallas_call x5, Pallas kernels, backward_call(): pl.pallas_call(partial(backward_kernel, sizes=tuple((piece[2] for piece i...  52.8 us
    ppermute x4, waiting for transfers between devices, swap_unit(): return lax.ppermute(value, 'unit', [(0, 1), (1, 0)])  49.5 us
    pallas_call x5, Pallas kernels, forward_call(): pl.pallas_call(partial(forward_kernel, sizes=tuple((piece[2] for piece in...  39.6 us
    ppermute x26, starting transfers between devices, partner(): return lax.ppermute(value, axis, pairs)  31.8 us
  transfers between devices with their start and end apart: 31, of which 14 were waited for; matrix products, arithmetic and copies ran while one was open for 25% of the time, Pallas kernels for 18%

profile of v1, /device:TPU:1, one launch (start us, length us, event | category | flops | bytes accessed | tf_op | source)
XLA Modules:
  0.0 562.3 jit_solution(9893259510002067452)
XLA Ops:
  13.4 10.0 %project.1 = (bf16[8,144,1024]{2,1,0:T(8,128)(2,1)}, bf16[8,144,1024]{2,1,0:T(8,128)(2,1)}, bf16[768,1024]{1,0:T(8,128)(2,1)}) custom-call(s32[2]{0:T(128)} %pad_add_fusion.pos_ref, bf16[1024,768]{1,0:T(8,128)(2,1)} %tok_ref.1, f32[1,768]{1,0:T(1,128)} %broadcast_in_dim.70.gain_ref, f32[1,768]{1,0:T(1,128)} %broadcast_in_dim.71.shift_ref, ...), custom_call_target="tpu_custom_call" | custom-call | flops 3422552064 | bytes 12582912 | tf_op jit(solution)/shard_map/project/pallas_call | solution.py:536
  28.2 8.8 %reshape.143 = s32[16,64,2,2,2,2]{5,4,3,2,1,0:T(2,128)} reshape(s32[16384]{0:T(1024)} %fusion.57) | data formatting | bytes 131072 | tf_op jit(solution)/shard_map/reshape | solution.py:981
  37.0 6.4 %copy.46 = s32[16,2,2,2,2,64]{5,4,3,2,1,0:T(2,128)} copy(s32[16,2,2,2,2,64]{1,2,3,4,5,0:T(2,128)} %bitcast.50) | data formatting | bytes 131072 | tf_op jit(solution)/shard_map/transpose | solution.py:982
  77.1 9.6 %attend1.1 = bf16[4,64,1024]{2,1,0:T(8,128)(2,1)} custom-call(bf16[8,144,1024]{2,1,0:T(8,128)(2,1)} %get-tuple-element.31.refs_0_, bf16[4,144,960]{2,1,0:T(8,128)(2,1)} %copy-done.6, s32[4,1,1024]{2,1,0:T(1,128)} %copy-done.56), custom_call_target="tpu_custom_call" | custom-call | flops 4294967296 | bytes 2097152 | tf_op jit(solution)/shard_map/attend1/pallas_call | solution.py:692
  91.7 5.6 attend2.1
  125.4 18.0 %attend0.1 = (f32[8,48,1024]{2,1,0:T(8,128)}, f32[8,1,1024]{2,1,0:T(1,128)}) custom-call(bf16[8,144,1024]{2,1,0:T(8,128)(2,1)} %get-tuple-element.28.refs_0_, s32[8,1,1024]{2,1,0:T(1,128)} %broadcast_in_dim.78.refs_1_.refs_2_), custom_call_target="tpu_custom_call" | custom-call | flops 8589934592 | bytes 4194304 | tf_op jit(solution)/shard_map/attend0/pallas_call | solution.py:692
  157.2 5.0 convolution_convert_fusion.5
  162.3 26.2 %collective-permute-done.7 = bf16[1024,768]{0,1:T(8,128)(2,1)S(1)} collective-permute-done((bf16[1024,768]{0,1:T(8,128)(2,1)S(1)}, bf16[1024,768]{0,1:T(8,128)(2,1)S(1)}, u32[]{:S(2)}, u32[]{:S(2)}) %collective-permute-start.7) | collective-permute-done | bytes 1572896 | tf_op jit(solution)/shard_map/ppermute | solution.py:874
  195.5 9.3 %convert_reduce_fusion = (f32[1536]{0:T(1024)}, bf16[1024,1536]{1,0:T(8,128)(2,1)S(1)}) fusion(f32[1024,1536]{1,0:T(8,128)S(1)} %fusion.109, f32[1536]{0:T(1024)S(1)} %copy-done.64, bf16[1024,768]{0,1:T(8,128)(2,1)S(1)} %convolution_convert_fusion.5, bf16[1536,768]{1,0:T(8,128)(2,1)S(1)} %copy-done), kind=kOutput, calls=%fused_computation.19 | convolution fusion | flops 2458384896 | bytes 13381632 | tf_op jit(solution)/shard_map/dot_general | solution.py:1051
  213.5 5.7 %convolution_convert_fusion = bf16[1536,768]{1,0:T(8,128)(2,1)} fusion(bf16[1024,768]{0,1:T(8,128)(2,1)S(1)} %convolution_convert_fusion.5, f32[1024,1536]{1,0:T(8,128)S(1)} %fusion.109, f32[1536]{0:T(1024)S(1)} %copy-done.64), kind=kOutput, calls=%fused_computation.50 | convolution fusion | flops 2432827392 | bytes 10229760 | tf_op jit(solution)/shard_map/dot_general | solution.py:1058
  219.3 23.3 %collective-permute-done.9 = bf16[1024,768]{0,1:T(8,128)(2,1)S(1)} collective-permute-done((bf16[1024,768]{0,1:T(8,128)(2,1)S(1)}, bf16[1024,768]{0,1:T(8,128)(2,1)S(1)}, u32[]{:S(2)}, u32[]{:S(2)}) %collective-permute-start.9) | collective-permute-done | bytes 1572896 | tf_op jit(solution)/shard_map/ppermute | solution.py:874
  257.1 7.0 %convolution_convert_fusion.1 = bf16[768,1536]{1,0:T(8,128)(2,1)} fusion(bf16[1024,1536]{1,0:T(8,128)(2,1)} %copy-done.67, f32[1024,768]{0,1:T(8,128)} %copy-done.2, f32[768]{0:T(1024)S(1)} %copy-done.65, f32[768]{0:T(1024)S(1)} %copy-done.39, f32[1024]{0:T(1024)S(1)} %fusion.66, f32[1024]{0:T(1024)S(1)} %broadcast_multiply_fusion.1), kind=kOutput, calls=%fused_computation.51 | convolution fusion | flops 2421030912 | bytes 8665088 | tf_op jit(solution)/shard_map/dot_general | solution.py:1060
  268.7 13.2 %attend_back1.1 = bf16[4,144,1024]{2,1,0:T(8,128)(2,1)} custom-call(bf16[8,144,1024]{2,1,0:T(8,128)(2,1)} %get-tuple-element.31.refs_0_, bf16[4,144,960]{2,1,0:T(8,128)(2,1)} %copy-done.6, bf16[8,64,1024]{2,1,0:T(8,128)(2,1)} %get-tuple-element.35.refs_2_.refs_3_.refs_4_.refs_5_, bf16[4,64,960]{2,1,0:T(8,128)(2,1)} %copy-done.12, s32[4,1,1024]{2,1,0:T(1,128)} %copy-done.56), custom_call_target="tpu_custom_call" | custom-call | flops 6442450944 | bytes 4194304 | tf_op jit(solution)/shard_map/attend_back1/pallas_call | solution.py:716
  300.5 7.4 %attend_back2.1 = bf16[2,144,1024]{2,1,0:T(8,128)(2,1)} custom-call(bf16[8,144,1024]{2,1,0:T(8,128)(2,1)} %get-tuple-element.31.refs_0_, bf16[4,144,960]{2,1,0:T(8,128)(2,1)} %copy-done.6, bf16[2,144,896]{2,1,0:T(8,128)(2,1)} %collective-permute-done.1.refs_2_, bf16[8,64,1024]{2,1,0:T(8,128)(2,1)} %get-tuple-element.35.refs_2_.refs_3_.refs_4_.refs_5_, ...), custom_call_target="tpu_custom_call" | custom-call | flops 3221225472 | bytes 2097152 | tf_op jit(solution)/shard_map/attend_back2/pallas_call | solution.py:716
  312.8 8.5 %collective-permute-done.15 = bf16[2,144,896]{2,1,0:T(8,128)(2,1)S(1)} collective-permute-done((bf16[2,144,896]{2,1,0:T(8,128)(2,1)S(1)}, bf16[2,144,896]{2,1,0:T(8,128)(2,1)S(1)}, u32[]{:S(2)}, u32[]{:S(2)}) %collective-permute-start.15) | collective-permute-done | bytes 516128 | tf_op jit(solution)/shard_map/ppermute | solution.py:32
  325.6 24.4 %attend_back0.1.own_ref = f32[8,144,1024]{2,1,0:T(8,128)} custom-call(bf16[8,144,1024]{2,1,0:T(8,128)(2,1)} %get-tuple-element.28.refs_0_, bf16[8,64,1024]{2,1,0:T(8,128)(2,1)} %get-tuple-element.34.refs_1_, s32[8,1,1024]{2,1,0:T(1,128)} %broadcast_in_dim.78.refs_1_.refs_2_), custom_call_target="tpu_custom_call" | custom-call | flops 12884901888 | bytes 8388608 | tf_op jit(solution)/shard_map/attend_back0/pallas_call | solution.py:716
  353.1 5.8 %collect.1 = bf16[1152,1024]{1,0:T(8,128)(2,1)} custom-call(s32[2]{0:T(128)} %pad_add_fusion.pos_ref, f32[8,144,1024]{2,1,0:T(8,128)} %attend_back0.1.own_ref, bf16[8,144,960]{2,1,0:T(8,128)(2,1)} %pad_maximum_fusion.back_ref), custom_call_target="tpu_custom_call" | custom-call | flops 100000000 | bytes 9437184 | tf_op jit(solution)/shard_map/collect/pallas_call | solution.py:858
  376.6 16.9 %collective-permute-done.23 = bf16[192,1152]{1,0:T(8,128)(2,1)S(1)} collective-permute-done((bf16[192,1152]{1,0:T(8,128)(2,1)S(1)}, bf16[192,1152]{1,0:T(8,128)(2,1)S(1)}, u32[]{:S(2)}, u32[]{:S(2)}) %collective-permute-start.23) | collective-permute-done | bytes 442400 | tf_op jit(solution)/shard_map/ppermute | solution.py:32
  394.8 5.2 convolution_convert_fusion.6
  400.0 99.6 %all-reduce.3.cloned.1.call-done = (bf16[384,768]{1,0:T(8,128)(2,1)}, bf16[768,1536]{1,0:T(8,128)(2,1)}, bf16[1536,768]{1,0:T(8,128)(2,1)}) async-done(((bf16[384,768]{1,0:T(8,128)(2,1)}, bf16[768,1536]{1,0:T(8,128)(2,1)}, bf16[1536,768]{1,0:T(8,128)(2,1)}), (bf16[384,768]{1,0:T(8,128)(2,1)}, bf16[768,1536]{1,0:T(8,128)(2,1)}, bf16[1536,768]{1,0:T(8,128)(2,1)})) %all-reduce.3.cloned.1.call-update) | async-done | bytes 5308432 | tf_op jit(solution)/shard_map/psum | solution.py:1069
  501.7 4.6 convert_element_type.222
  521.6 6.2 %collective-permute-done.26 = bf16[48,1152]{1,0:T(8,128)(2,1)S(1)} collective-permute-done((bf16[48,1152]{1,0:T(8,128)(2,1)S(1)}, bf16[48,1152]{1,0:T(8,128)(2,1)S(1)}, u32[]{:S(2)}, u32[]{:S(2)}) %collective-permute-start.26) | collective-permute-done | bytes 110624 | tf_op jit(solution)/shard_map/ppermute | solution.py:32
  529.6 4.7 collective-permute-done.27
  538.4 5.9 %collective-permute-done.28 = bf16[192,1152]{1,0:T(8,128)(2,1)S(1)} collective-permute-done((bf16[192,1152]{1,0:T(8,128)(2,1)S(1)}, bf16[192,1152]{1,0:T(8,128)(2,1)S(1)}, u32[]{:S(2)}, u32[]{:S(2)}) %collective-permute-start.28) | collective-permute-done | bytes 442400 | tf_op jit(solution)/shard_map/ppermute | solution.py:32
  (376 shorter events, 209.6 us)
Async XLA Ops:
  7.2 492.3 %all-reduce.3.cloned.1.call-start = ((), (), s32[]{:S(2)}) async-start(), calls=%async_computation | async-start | bytes 10616832 | tf_op jit(solution)/shard_map/psum | solution.py:1069
  25.8 42.2 %collective-permute-start = (bf16[4,144,960]{2,1,0:T(8,128)(2,1)}, bf16[4,144,960]{2,1,0:T(8,128)(2,1)S(1)}, u32[]{:S(2)}, u32[]{:S(2)}) collective-permute-start(bf16[4,144,960]{2,1,0:T(8,128)(2,1)} %slice.335), channel_id=1, source_target_pairs={{0,1},{1,0},{2,3},{3,2},{4,5},{5,4},{6,7},{7,6},{8,9},{9,8},{10,11... | collective-permute-start | bytes 3317768 | tf_op jit(solution)/shard_map/ppermute | solution.py:32
  72.5 15.2 %collective-permute-start.1 = (bf16[2,144,896]{2,1,0:T(8,128)(2,1)}, bf16[2,144,896]{2,1,0:T(8,128)(2,1)}, u32[]{:S(2)}, u32[]{:S(2)}) collective-permute-start(bf16[2,144,896]{2,1,0:T(8,128)(2,1)} %concatenate.123), channel_id=1, source_target_pairs={{0,2},{1,3},{2,0},{3,1},{4,6},{5,7},{6,4},{7,5},{8,10},{9,11},{10,... | collective-permute-start | bytes 1548296 | tf_op jit(solution)/shard_map/ppermute | solution.py:32
  90.4 8.6 %collective-permute-start.2 = (bf16[1,144,768]{2,1,0:T(8,128)(2,1)S(1)}, bf16[1,144,768]{2,1,0:T(8,128)(2,1)S(1)}, u32[]{:S(2)}, u32[]{:S(2)}) collective-permute-start(bf16[1,144,768]{2,1,0:T(8,128)(2,1)S(1)} %concatenate.124), channel_id=1, source_target_pairs={{0,4},{1,5},{2,6},{3,7},{4,0},{5,1},{6,2},{7,3},{8,12},{9,13},{10,... | collective-permute-start | bytes 663560 | tf_op jit(solution)/shard_map/ppermute | solution.py:32
  99.7 7.8 %collective-permute-start.3 = (bf16[1,96,512]{2,1,0:T(8,128)(2,1)}, bf16[1,96,512]{2,1,0:T(8,128)(2,1)S(1)}, u32[]{:S(2)}, u32[]{:S(2)}) collective-permute-start(bf16[1,96,512]{2,1,0:T(8,128)(2,1)} %pad_maximum_fusion.3), channel_id=1, source_target_pairs={{0,8},{1,9},{2,10},{3,11},{4,12},{5,13},{6,14},{7,15},{8,0},{9,1},... | collective-permute-start | bytes 294920 | tf_op jit(solution)/shard_map/ppermute | solution.py:32
  122.4 20.9 %collective-permute-start.6 = (bf16[4,64,960]{2,1,0:T(8,128)(2,1)}, bf16[4,64,960]{2,1,0:T(8,128)(2,1)}, u32[]{:S(2)}, u32[]{:S(2)}) collective-permute-start(bf16[4,64,960]{2,1,0:T(8,128)(2,1)} %maximum_maximum_fusion), channel_id=1, source_target_pairs={{0,1},{1,0},{2,3},{3,2},{4,5},{5,4},{6,7},{7,6},{8,9},{9,8},{10,11... | collective-permute-start | bytes 1474568 | tf_op jit(solution)/shard_map/ppermute | solution.py:32
  152.4 36.1 %collective-permute-start.7 = (bf16[1024,768]{0,1:T(8,128)(2,1)S(1)}, bf16[1024,768]{0,1:T(8,128)(2,1)S(1)}, u32[]{:S(2)}, u32[]{:S(2)}) collective-permute-start(bf16[1024,768]{0,1:T(8,128)(2,1)S(1)} %convolution_convert_fusion.3), channel_id=1, source_target_pairs={{0,16},{16,0},{1,17},{17,1},{2,18},{18,2},{3,19},{19,3},{4,20},{20... | collective-permute-start | bytes 4718600 | tf_op jit(solution)/shard_map/ppermute | solution.py:874
  207.4 35.2 %collective-permute-start.9 = (bf16[1024,768]{0,1:T(8,128)(2,1)S(1)}, bf16[1024,768]{0,1:T(8,128)(2,1)S(1)}, u32[]{:S(2)}, u32[]{:S(2)}) collective-permute-start(bf16[1024,768]{0,1:T(8,128)(2,1)S(1)} %convolution_convert_fusion.4), channel_id=1, source_target_pairs={{0,16},{16,0},{1,17},{17,1},{2,18},{18,2},{3,19},{19,3},{4,20},{20... | collective-permute-start | bytes 4718600 | tf_op jit(solution)/shard_map/ppermute | solution.py:874
  212.6 182.1 %collective-permute-start.8 = (bf16[1024,768]{0,1:T(8,128)(2,1)}, bf16[1024,768]{0,1:T(8,128)(2,1)}, u32[]{:S(2)}, u32[]{:S(2)}) collective-permute-start(bf16[1024,768]{0,1:T(8,128)(2,1)} %convolution_convert_fusion.7), channel_id=1, source_target_pairs={{0,16},{16,0},{1,17},{17,1},{2,18},{18,2},{3,19},{19,3},{4,20},{20... | collective-permute-start | bytes 4718600 | tf_op jit(solution)/shard_map/ppermute | solution.py:874
  254.1 13.8 %collective-permute-start.10 = (bf16[4,64,960]{2,1,0:T(8,128)(2,1)S(1)}, bf16[4,64,960]{2,1,0:T(8,128)(2,1)S(1)}, u32[]{:S(2)}, u32[]{:S(2)}) collective-permute-start(bf16[4,64,960]{2,1,0:T(8,128)(2,1)S(1)} %slice.380), channel_id=1, source_target_pairs={{0,1},{1,0},{2,3},{3,2},{4,5},{5,4},{6,7},{7,6},{8,9},{9,8},{10,11... | collective-permute-start | bytes 1474568 | tf_op jit(solution)/shard_map/ppermute | solution.py:32
  268.1 15.3 %collective-permute-start.11 = (bf16[2,64,896]{2,1,0:T(8,128)(2,1)S(1)}, bf16[2,64,896]{2,1,0:T(8,128)(2,1)S(1)}, u32[]{:S(2)}, u32[]{:S(2)}) collective-permute-start(bf16[2,64,896]{2,1,0:T(8,128)(2,1)S(1)} %concatenate.139), channel_id=1, source_target_pairs={{0,2},{1,3},{2,0},{3,1},{4,6},{5,7},{6,4},{7,5},{8,10},{9,11},{10,... | collective-permute-start | bytes 688136 | tf_op jit(solution)/shard_map/ppermute | solution.py:32
  292.4 7.5 %collective-permute-start.13 = (bf16[1,96,512]{2,1,0:T(8,128)(2,1)}, bf16[1,96,512]{2,1,0:T(8,128)(2,1)S(1)}, u32[]{:S(2)}, u32[]{:S(2)}) collective-permute-start(bf16[1,96,512]{2,1,0:T(8,128)(2,1)} %get-tuple-element.37), channel_id=1, source_target_pairs={{0,8},{1,9},{2,10},{3,11},{4,12},{5,13},{6,14},{7,15},{8,0},{9,1},... | collective-permute-start | bytes 294920 | tf_op jit(solution)/shard_map/ppermute | solution.py:32
  300.0 8.9 %collective-permute-start.14 = (bf16[1,144,768]{2,1,0:T(8,128)(2,1)S(1)}, bf16[1,144,768]{2,1,0:T(8,128)(2,1)S(1)}, u32[]{:S(2)}, u32[]{:S(2)}) collective-permute-start(bf16[1,144,768]{2,1,0:T(8,128)(2,1)S(1)} %pad_maximum_fusion.2), channel_id=1, source_target_pairs={{0,4},{1,5},{2,6},{3,7},{4,0},{5,1},{6,2},{7,3},{8,12},{9,13},{10,... | collective-permute-start | bytes 663560 | tf_op jit(solution)/shard_map/ppermute | solution.py:32
  309.6 11.6 %collective-permute-start.15 = (bf16[2,144,896]{2,1,0:T(8,128)(2,1)S(1)}, bf16[2,144,896]{2,1,0:T(8,128)(2,1)S(1)}, u32[]{:S(2)}, u32[]{:S(2)}) collective-permute-start(bf16[2,144,896]{2,1,0:T(8,128)(2,1)S(1)} %maximum_maximum_fusion.1), channel_id=1, source_target_pairs={{0,2},{1,3},{2,0},{3,1},{4,6},{5,7},{6,4},{7,5},{8,10},{9,11},{10,... | collective-permute-start | bytes 1548296 | tf_op jit(solution)/shard_map/ppermute | solution.py:32
  322.9 27.1 %collective-permute-start.16 = (bf16[4,144,960]{2,1,0:T(8,128)(2,1)S(1)}, bf16[4,144,960]{2,1,0:T(8,128)(2,1)}, u32[]{:S(2)}, u32[]{:S(2)}) collective-permute-start(bf16[4,144,960]{2,1,0:T(8,128)(2,1)S(1)} %fusion.46), channel_id=1, source_target_pairs={{0,1},{1,0},{2,3},{3,2},{4,5},{5,4},{6,7},{7,6},{8,9},{9,8},{10,11... | collective-permute-start | bytes 3317768 | tf_op jit(solution)/shard_map/ppermute | solution.py:32
  372.2 21.3 %collective-permute-start.23 = (bf16[192,1152]{1,0:T(8,128)(2,1)S(1)}, bf16[192,1152]{1,0:T(8,128)(2,1)S(1)}, u32[]{:S(2)}, u32[]{:S(2)}) collective-permute-start(bf16[192,1152]{1,0:T(8,128)(2,1)S(1)} %constant_dynamic-slice_fusion.2), channel_id=1, source_target_pairs={{0,2},{1,3},{2,0},{3,1},{4,6},{5,7},{6,4},{7,5},{8,10},{9,11},{10,... | collective-permute-start | bytes 1327112 | tf_op jit(solution)/shard_map/ppermute | solution.py:32
  375.4 136.2 %collective-permute-start.17 = (bf16[1024,768]{0,1:T(8,128)(2,1)}, bf16[1024,768]{0,1:T(8,128)(2,1)}, u32[]{:S(2)}, u32[]{:S(2)}) collective-permute-start(bf16[1024,768]{0,1:T(8,128)(2,1)} %add_convert_fusion), channel_id=1, source_target_pairs={{0,16},{16,0},{1,17},{17,1},{2,18},{18,2},{3,19},{19,3},{4,20},{20... | collective-permute-start | bytes 4718600 | tf_op jit(solution)/shard_map/ppermute | solution.py:874
  393.7 115.6 %collective-permute-start.24 = (bf16[96,1152]{1,0:T(8,128)(2,1)S(1)}, bf16[96,1152]{1,0:T(8,128)(2,1)S(1)}, u32[]{:S(2)}, u32[]{:S(2)}) collective-permute-start(bf16[96,1152]{1,0:T(8,128)(2,1)S(1)} %constant_dynamic-slice_fusion.1), channel_id=1, source_target_pairs={{0,4},{1,5},{2,6},{3,7},{4,0},{5,1},{6,2},{7,3},{8,12},{9,13},{10,... | collective-permute-start | bytes 663560 | tf_op jit(solution)/shard_map/ppermute | solution.py:32
  509.4 10.2 %collective-permute-start.25 = (bf16[48,1152]{1,0:T(8,128)(2,1)S(1)}, bf16[48,1152]{1,0:T(8,128)(2,1)S(1)}, u32[]{:S(2)}, u32[]{:S(2)}) collective-permute-start(bf16[48,1152]{1,0:T(8,128)(2,1)S(1)} %constant_dynamic-slice_fusion), channel_id=1, source_target_pairs={{0,8},{1,9},{2,10},{3,11},{4,12},{5,13},{6,14},{7,15},{8,0},{9,1},... | collective-permute-start | bytes 331784 | tf_op jit(solution)/shard_map/ppermute | solution.py:32
  519.6 8.2 %collective-permute-start.26 = (bf16[48,1152]{1,0:T(8,128)(2,1)S(1)}, bf16[48,1152]{1,0:T(8,128)(2,1)S(1)}, u32[]{:S(2)}, u32[]{:S(2)}) collective-permute-start(bf16[48,1152]{1,0:T(8,128)(2,1)S(1)} %add_convert_fusion.7), channel_id=1, source_target_pairs={{0,8},{1,9},{2,10},{3,11},{4,12},{5,13},{6,14},{7,15},{8,0},{9,1},... | collective-permute-start | bytes 331784 | tf_op jit(solution)/shard_map/ppermute | solution.py:32
  527.9 9.8 %collective-permute-start.20 = (f32[54,128]{1,0:T(8,128)S(1)}, f32[54,128]{1,0:T(8,128)S(1)}, u32[]{:S(2)}, u32[]{:S(2)}) collective-permute-start(f32[54,128]{1,0:T(8,128)S(1)} %fusion.155), channel_id=1, source_target_pairs={{0,4},{1,5},{2,6},{3,7},{4,0},{5,1},{6,2},{7,3},{8,12},{9,13},{10,... | collective-permute-start | bytes 82952 | tf_op jit(solution)/shard_map/ppermute | solution.py:32
  534.3 10.0 %collective-permute-start.28 = (bf16[192,1152]{1,0:T(8,128)(2,1)S(1)}, bf16[192,1152]{1,0:T(8,128)(2,1)S(1)}, u32[]{:S(2)}, u32[]{:S(2)}) collective-permute-start(bf16[192,1152]{1,0:T(8,128)(2,1)S(1)} %maximum_select_fusion.2), channel_id=1, source_target_pairs={{0,2},{1,3},{2,0},{3,1},{4,6},{5,7},{6,4},{7,5},{8,10},{9,11},{10,... | collective-permute-start | bytes 1327112 | tf_op jit(solution)/shard_map/ppermute | solution.py:32
  537.7 13.4 %collective-permute-start.21 = (f32[54,128]{1,0:T(8,128)S(1)}, f32[54,128]{1,0:T(8,128)S(1)}, u32[]{:S(2)}, u32[]{:S(2)}) collective-permute-start(f32[54,128]{1,0:T(8,128)S(1)} %add.399), channel_id=1, source_target_pairs={{0,8},{1,9},{2,10},{3,11},{4,12},{5,13},{6,14},{7,15},{8,0},{9,1},... | collective-permute-start | bytes 82952 | tf_op jit(solution)/shard_map/ppermute | solution.py:32
  544.6 8.3 %collective-permute-start.29 = (bf16[384,1152]{1,0:T(8,128)(2,1)S(1)}, bf16[384,1152]{1,0:T(8,128)(2,1)S(1)}, u32[]{:S(2)}, u32[]{:S(2)}) collective-permute-start(bf16[384,1152]{1,0:T(8,128)(2,1)S(1)} %maximum_select_fusion.1), channel_id=1, source_target_pairs={{0,1},{1,0},{2,3},{3,2},{4,5},{5,4},{6,7},{7,6},{8,9},{9,8},{10,11... | collective-permute-start | bytes 2654216 | tf_op jit(solution)/shard_map/ppermute | solution.py:32
  (80 other events, 1285.2 us)
Sparse Core Ops, SparseCore 0:
  366.7 132.7 all-reduce.2

commit v2 on v1

--- a/solution.py
+++ b/solution.py
@@ -486,15 +486,41 @@
     return lax.broadcasted_iota(jnp.int32, (count, lanes), 0)
 
 
+def column(vector):
+    return jnp.broadcast_to(vector[None, :], (8, vector.shape[0])).T[:, :1]
+
+
 def project_kernel(
-    pos_ref, tok_ref, gain_ref, shift_ref, wq_ref, bq_ref, wk_ref, wv_ref, bv_ref, all_ref, send_ref, normed_ref
+    pos_ref,
+    tok_ref,
+    doc_ref,
+    valid_ref,
+    gain_ref,
+    shift_ref,
+    wq_ref,
+    bq_ref,
+    wk_ref,
+    wv_ref,
+    bv_ref,
+    all_ref,
+    own_ref,
+    away_ref,
+    normed_ref,
+    tags0_ref,
+    tags1_ref,
+    tags2_ref,
+    tags3_ref,
+    tags4_ref,
+    place_ref,
 ):
     dl = pos_ref[0]
     unit = pos_ref[1]
+    device = pos_ref[2]
     values = tok_ref[...].astype(F32)
     centred = values - jnp.mean(values, axis=-1, keepdims=True)
     row_var = jnp.mean(centred * centred, axis=-1, keepdims=True)
-    normed = (centred * lax.rsqrt(row_var + EPSILON) * gain_ref[...] + shift_ref[...]).astype(BF16)
+    scaled = centred * lax.rsqrt(row_var + EPSILON)
+    normed = (scaled * gain_ref[...][None, :] + shift_ref[...][None, :]).astype(BF16)
     order = one_hot_rows(False)
     normed_t = lax.dot_general(normed, order, TN, preferred_element_type=F32).astype(BF16)
     normed_ref[...] = normed_t
@@ -502,51 +528,98 @@
     def project(w_ref):
         return lax.dot_general(w_ref[...], normed_t, TN, preferred_element_type=F32)
 
-    query = ((project(wq_ref) + bq_ref[...]) * HEAD_DIM**-0.5).astype(BF16)
+    query = ((project(wq_ref) + column(bq_ref[...])) * HEAD_DIM**-0.5).astype(BF16)
     key = project(wk_ref).astype(BF16)
-    value = (project(wv_ref) + bv_ref[...]).astype(BF16)
+    value = (project(wv_ref) + column(bv_ref[...])).astype(BF16)
     for head in range(HEADS_HERE):
         own = slice(head * HEAD_DIM, (head + 1) * HEAD_DIM)
-        for at, part in enumerate((query, key, value)):
-            rows = slice(at * HEAD_DIM, (at + 1) * HEAD_DIM)
-            here = part[own]
-            all_ref[head, rows, :] = here
+        heres = [part[own] for part in (query, key, value)]
+        for at, here in enumerate(heres):
+            all_ref[head, at * HEAD_DIM : (at + 1) * HEAD_DIM, :] = here
+        store_classes(head, unit, dl, heres, own_ref, away_ref)
+
+    tags = jnp.where(valid_ref[...] == 1, doc_ref[...] + 1, 0)
+    rows = jnp.concatenate([tags[:, at * SEG0 : (at + 1) * SEG0] for at in range(16)], axis=0)
+    placed = jnp.dot(rows.astype(F32).astype(BF16), order, preferred_element_type=F32)
+    place_ref[...] = placed.astype(jnp.int32)
+    relative = [place_ref[pl.ds(at ^ device, 1), :] for at in range(16)]
+    tags0_ref[...] = relative[0]
+    for branch, ref in ((1, tags1_ref), (2, tags2_ref), (3, tags3_ref), (4, tags4_ref)):
+        heads = 8 >> min(branch, 3)
+        for head in range(HEADS_HERE):
+
+            @pl.when((head ^ dl) < heads)
+            def _():
+                blocks = [row[:, class_lanes(head, min(branch, 3))] for row in relative[: 2**branch]]
+                if branch == 4:
+                    blocks = [jnp.where(unit == 0, block[:, :64], block[:, 64:]) for block in blocks]
+                ref[head ^ dl] = jnp.concatenate(blocks, axis=1)
+
+
+def store_classes(head, unit, dl, heres, own_ref, away_ref):
+    at = head ^ dl
+
+    def store(ref):
+        start_row = 0
+        for here in heres:
+            rows = slice(start_row, start_row + here.shape[0])
+            start_row += here.shape[0]
             for branch in (1, 2, 3):
                 start, size = LANES0[branch]
-                send_ref[head ^ dl, rows, start : start + size] = here[:, class_lanes(head, branch)]
+                ref[at & 3, rows, start : start + size] = here[:, class_lanes(head, branch)]
             both = here[:, class_lanes(head, 3)]
             picked = jnp.where(unit == 0, both[:, :64].astype(F32), both[:, 64:].astype(F32))
-            send_ref[head ^ dl, rows, 896:960] = picked.astype(BF16)
-            send_ref[head ^ dl, rows, 960:1024] = jnp.zeros((HEAD_DIM, 64), BF16)
+            ref[at & 3, rows, 896:960] = picked.astype(BF16)
+
+    @pl.when(at < 4)
+    def _():
+        store(own_ref)
+
+    @pl.when(at >= 4)
+    def _():
+        store(away_ref)
 
 
 def whole_spec(shape):
     return pl.BlockSpec(shape, lambda *_: (0,) * len(shape))
 
 
-def project_call(place, tokens, gain, shift, w_query, b_query, w_key, w_value, b_value):
-    width = HEADS_HERE * HEAD_DIM
-    model = tokens.shape[1]
-    args = (tokens, gain[None], shift[None], w_query, b_query[:, None], w_key, w_value, b_value[:, None])
-    out_shape = [
-        jax.ShapeDtypeStruct((HEADS_HERE, QKV, SEG0), BF16),
-        jax.ShapeDtypeStruct((HEADS_HERE, QKV, SEG0), BF16),
-        jax.ShapeDtypeStruct((model, SEG0), BF16),
-    ]
+def whole_call(kernel, name, place, args, out_shape, scratch=(), flops=10**8, transcendentals=0):
+    moved = sum(math.prod(a.shape) * a.dtype.itemsize for a in list(args) + list(out_shape))
     return pl.pallas_call(
-        project_kernel,
+        kernel,
         grid_spec=pltpu.PrefetchScalarGridSpec(
             num_scalar_prefetch=1,
             grid=(1,),
             in_specs=[whole_spec(a.shape) for a in args],
             out_specs=[whole_spec(o.shape) for o in out_shape],
+            scratch_shapes=scratch,
         ),
         out_shape=out_shape,
-        name="project",
-        cost_estimate=pl.CostEstimate(
-            flops=2 * SEG0 * model * (3 * width + SEG0), bytes_accessed=12 * 2**20, transcendentals=SEG0
-        ),
+        name=name,
+        cost_estimate=pl.CostEstimate(flops=flops, bytes_accessed=moved, transcendentals=transcendentals),
     )(place, *args)
+
+
+def project_call(place, *args):
+    width = HEADS_HERE * HEAD_DIM
+    model = args[0].shape[1]
+    out_shape = [
+        jax.ShapeDtypeStruct((HEADS_HERE, QKV, SEG0), BF16),
+        jax.ShapeDtypeStruct((4, QKV, 960), BF16),
+        jax.ShapeDtypeStruct((4, QKV, 960), BF16),
+        jax.ShapeDtypeStruct((model, SEG0), BF16),
+        jax.ShapeDtypeStruct((1, SEG0), jnp.int32),
+    ] + [jax.ShapeDtypeStruct((8 >> min(branch, 3), 1, SEG0), jnp.int32) for branch in range(1, 5)]
+    return whole_call(
+        project_kernel,
+        "project",
+        place,
+        args,
+        out_shape,
+        scratch=[pltpu.VMEM((16, SEG0), jnp.int32)],
+        flops=2 * SEG0 * model * (3 * width + SEG0),
+    )
 
 
 def key_tail(tags):
@@ -577,7 +650,7 @@
         last = piece_refs[-1]
         key = jnp.concatenate([key, last[0, :HEAD_DIM, :]], axis=1)
         value = jnp.concatenate([value, last[0, HEAD_DIM : 2 * HEAD_DIM, :]], axis=1)
-    tags = tag_ref[0]
+    tags = tag_ref[...].reshape(1, SEG0)
     keys = key.shape[1]
     key_rows = jnp.concatenate([key, key_tail(tags)], axis=0).T
     ones = jnp.where(rows_iota(AUG, keys) == 0, 1.0, 0.0).astype(BF16)
@@ -623,7 +696,7 @@
     grad_pieces = [(grad_refs[i], grad_sizes[i]) for i in range(grads)]
     grad = gather_rows(grad_pieces, (0, HEAD_DIM))
     tail = gather_rows(grad_pieces, (HEAD_DIM, OUT_ROWS)).astype(F32)
-    tags = tag_ref[0]
+    tags = tag_ref[...].reshape(1, SEG0)
     keys, queries = key.shape[1], query.shape[1]
     key_rows = jnp.concatenate([key, key_tail(tags)], axis=0).T
     ones = jnp.where(rows_iota(AUG, keys) < 3, 1.0, 0.0).astype(BF16)
@@ -659,6 +732,12 @@
     return pl.BlockSpec((1, rows, block), lambda head, at=start // block: (head, 0, at))
 
 
+def tag_spec(branch):
+    if branch == 0:
+        return whole_spec((1, SEG0))
+    return pl.BlockSpec((1, 1, SEG0), lambda head: (head, 0, 0))
+
+
 def branch_pieces(branch, parts):
     if branch == 0:
         return [(parts[0], 0, SEG0)]
@@ -693,7 +772,7 @@
         partial(forward_kernel, sizes=tuple(piece[2] for piece in pieces), tile=512, packed=packed),
         grid=(heads,),
         in_specs=[lane_spec(array.shape[1], start, size) for array, start, size in pieces]
-        + [pl.BlockSpec((1, 1, SEG0), lambda head: (head, 0, 0))],
+        + [tag_spec(branch)],
         out_specs=out_specs,
         out_shape=out_shape,
         name=f"attend{branch}",
@@ -723,7 +802,7 @@
         ),
         grid=(heads,),
         in_specs=[lane_spec(array.shape[1], start, size) for array, start, size in pieces + grad_pieces]
-        + [pl.BlockSpec((1, 1, SEG0), lambda head: (head, 0, 0))],
+        + [tag_spec(branch)],
         out_specs=[pl.BlockSpec((1,) + out.shape[1:], lambda head: (head, 0, 0)) for out in out_shape],
         out_shape=out_shape,
         name=f"attend_back{branch}",
@@ -731,6 +810,20 @@
             flops=heads * queries * SEG0 * 2 * 768, bytes_accessed=heads * SEG0 * 1024, transcendentals=heads * queries * SEG0
         ),
     )(*[piece[0] for piece in pieces + grad_pieces], tags)
+
+
+def assemble(outs, third, second, first, full_ref):
+    out1, out2, out3, out4 = outs
+    full_ref[0:4, :, 0:512] = out1[:, :, 0:512]
+    full_ref[0:2, :, 512:768] = out2[:, :, 0:256]
+    full_ref[2:4, :, 512:768] = second[:, :, 0:256]
+    full_ref[0:1, :, 768:896] = out3[:, :, 0:128]
+    full_ref[1:2, :, 768:896] = third[:, :, 0:128]
+    full_ref[2:4, :, 768:896] = second[:, :, 512:640]
+    full_ref[0:1, :, 896:960] = out4[:, :, 0:64]
+    full_ref[1:2, :, 896:960] = third[:, :, 512:576]
+    full_ref[2:4, :, 896:960] = second[:, :, 768:832]
+    full_ref[4:8, :, 0:960] = first[...]
 
 
 def branch_blocks(head, unit, ref, rows, at):
@@ -745,21 +838,21 @@
     return blocks
 
 
-def merge_kernel(pos_ref, o_ref, lse_ref, back_ref, merged_ref, total_ref):
+def merge_kernel(
+    pos_ref, o_ref, lse_ref, out1, out2, out3, out4, third, second, first, merged_ref, low_ref, total_ref, back_ref
+):
     dl = pos_ref[0]
     unit = pos_ref[1]
+    assemble((out1, out2, out3, out4), third, second, first, back_ref)
     for head in range(HEADS_HERE):
         at = head ^ dl
-        peak = lse_ref[head]
         tails = branch_blocks(head, unit, back_ref, (HEAD_DIM, OUT_ROWS), at)
-        lses = []
+        full = [lse_ref[head]]
         for block in tails:
+            lanes = block[0]
             value = block[1][0:1] + block[1][1:2] + block[1][2:3]
             if len(block) == 3:
                 value = jnp.where(block[2][0:1], value, MASKED)
-            lses.append((block[0], value))
-        full = [lse_ref[head]]
-        for lanes, value in lses:
             pad = []
             if lanes.start:
                 pad.append(jnp.full((1, lanes.start), MASKED, F32))
@@ -777,27 +870,21 @@
         outs = branch_blocks(head, unit, back_ref, (0, HEAD_DIM), at)
         for block, share in zip(outs, shares[1:]):
             merged_ref[rows, block[0]] += block[1] * share[:, block[0]]
-
-
-def merge_call(place, outputs, lse, back):
+        low_ref[rows, :] = merged_ref[rows, :].astype(BF16)
+
+
+def merge_call(place, outputs, lse, backs):
     width = HEADS_HERE * HEAD_DIM
-    out_shape = [jax.ShapeDtypeStruct((width, SEG0), F32), jax.ShapeDtypeStruct((HEADS_HERE, 1, SEG0), F32)]
-    args = (outputs, lse, back)
-    return pl.pallas_call(
-        merge_kernel,
-        grid_spec=pltpu.PrefetchScalarGridSpec(
-            num_scalar_prefetch=1,
-            grid=(1,),
-            in_specs=[whole_spec(a.shape) for a in args],
-            out_specs=[whole_spec(o.shape) for o in out_shape],
-        ),
-        out_shape=out_shape,
-        name="merge",
-        cost_estimate=pl.CostEstimate(flops=10**8, bytes_accessed=6 * 2**20, transcendentals=SEG0 * 8),
-    )(place, *args)
-
-
-def spread_kernel(pos_ref, grad_ref, merged_ref, total_ref, all_ref, send_ref):
+    out_shape = [
+        jax.ShapeDtypeStruct((width, SEG0), F32),
+        jax.ShapeDtypeStruct((width, SEG0), BF16),
+        jax.ShapeDtypeStruct((HEADS_HERE, 1, SEG0), F32),
+    ]
+    scratch = [pltpu.VMEM((HEADS_HERE, OUT_ROWS, SEG0), BF16)]
+    return whole_call(merge_kernel, "merge", place, (outputs, lse) + backs, out_shape, scratch)
+
+
+def spread_kernel(pos_ref, grad_ref, merged_ref, total_ref, all_ref, own_ref, away_ref):
     dl = pos_ref[0]
     unit = pos_ref[1]
     at = rows_iota(AUG, SEG0)
@@ -809,40 +896,26 @@
         tail = jnp.zeros((AUG, SEG0), F32)
         for row, part in zip((0, 1, 2, 13, 14, 15), parts):
             tail = jnp.where(at == row, part, tail)
-        for place, here in ((slice(0, HEAD_DIM), grad), (slice(HEAD_DIM, OUT_ROWS), tail.astype(BF16))):
-            all_ref[head, place, :] = here
-            for branch in (1, 2, 3):
-                start, size = LANES0[branch]
-                send_ref[head ^ dl, place, start : start + size] = here[:, class_lanes(head, branch)]
-            both = here[:, class_lanes(head, 3)]
-            picked = jnp.where(unit == 0, both[:, :64].astype(F32), both[:, 64:].astype(F32))
-            send_ref[head ^ dl, place, 896:960] = picked.astype(BF16)
-            send_ref[head ^ dl, place, 960:1024] = jnp.zeros((here.shape[0], 64), BF16)
+        heres = (grad, tail.astype(BF16))
+        all_ref[head, :HEAD_DIM, :] = heres[0]
+        all_ref[head, HEAD_DIM:, :] = heres[1]
+        store_classes(head, unit, dl, heres, own_ref, away_ref)
 
 
 def spread_call(place, grad, merged, total):
-    out_shape = [jax.ShapeDtypeStruct((HEADS_HERE, OUT_ROWS, SEG0), BF16)] * 2
-    args = (grad, merged, total)
-    return pl.pallas_call(
-        spread_kernel,
-        grid_spec=pltpu.PrefetchScalarGridSpec(
-            num_scalar_prefetch=1,
-            grid=(1,),
-            in_specs=[whole_spec(a.shape) for a in args],
-            out_specs=[whole_spec(o.shape) for o in out_shape],
-        ),
-        out_shape=out_shape,
-        name="spread",
-        cost_estimate=pl.CostEstimate(flops=10**8, bytes_accessed=5 * 2**20, transcendentals=0),
-    )(place, *args)
-
-
-def collect_kernel(pos_ref, own_ref, back_ref, out_ref, sum_ref):
+    out_shape = [jax.ShapeDtypeStruct((HEADS_HERE, OUT_ROWS, SEG0), BF16)] + [
+        jax.ShapeDtypeStruct((4, OUT_ROWS, 960), BF16)
+    ] * 2
+    return whole_call(spread_kernel, "spread", place, (grad, merged, total), out_shape)
+
+
+def collect_kernel(pos_ref, grad_ref, out1, out2, out3, out4, third, second, first, out_ref, sum_ref, back_ref):
     dl = pos_ref[0]
     unit = pos_ref[1]
     width = HEADS_HERE * HEAD_DIM
+    assemble((out1, out2, out3, out4), third, second, first, back_ref)
     for head in range(HEADS_HERE):
-        sum_ref[...] = own_ref[head]
+        sum_ref[...] = grad_ref[head]
         for block in branch_blocks(head, unit, back_ref, (0, QKV), head ^ dl):
             value = block[1] if len(block) == 2 else jnp.where(block[2], block[1], 0.0)
             sum_ref[:, block[0]] += value
@@ -852,106 +925,105 @@
             ].astype(BF16)
 
 
-def collect_call(place, own, back):
-    out_shape = jax.ShapeDtypeStruct((HEADS_HERE * QKV, SEG0), BF16)
-    args = (own, back)
-    return pl.pallas_call(
-        collect_kernel,
-        grid_spec=pltpu.PrefetchScalarGridSpec(
-            num_scalar_prefetch=1,
-            grid=(1,),
-            in_specs=[whole_spec(a.shape) for a in args],
-            out_specs=whole_spec(out_shape.shape),
-            scratch_shapes=[pltpu.VMEM((QKV, SEG0), F32)],
-        ),
-        out_shape=out_shape,
-        name="collect",
-        cost_estimate=pl.CostEstimate(flops=10**8, bytes_accessed=9 * 2**20, transcendentals=0),
-    )(place, *args)
+def collect_call(place, own, backs):
+    out_shape = [jax.ShapeDtypeStruct((HEADS_HERE * QKV, SEG0), BF16)]
+    scratch = [pltpu.VMEM((QKV, SEG0), F32), pltpu.VMEM((HEADS_HERE, QKV, SEG0), BF16)]
+    return whole_call(collect_kernel, "collect", place, (own,) + backs, out_shape, scratch)[0]
 
 
 def swap_unit(value):
     return lax.ppermute(value, "unit", [(0, 1), (1, 0)])
 
 
-def cat(*parts):
-    return jnp.concatenate(parts, axis=2)
-
-
-def step1_rows(own, first):
-    return cat(
-        *[array[2:4, :, start : start + size] for start, size in (LANES0[2], LANES0[3], LANES0[4]) for array in (own, first)]
-    )
-
-
-def step2_rows(own, first, second):
-    pieces = []
+def copy_kernel(*refs, moves):
+    out_ref = refs[-1]
+    for source, heads_from, rows, lanes_from, heads_to, lanes_to in moves:
+        out_ref[heads_to, :, lanes_to] = refs[source][heads_from, rows, lanes_from]
+
+
+def pack(name, arrays, moves, shape):
+    def span(pair):
+        return slice(pair[0], pair[0] + pair[1])
+
+    moves = tuple((m[0], span(m[1]), span(m[2]), span(m[3]), span(m[4]), span(m[5])) for m in moves)
+    out = jax.ShapeDtypeStruct(shape, BF16)
+    return pl.pallas_call(
+        partial(copy_kernel, moves=moves),
+        out_shape=out,
+        name=name,
+        cost_estimate=pl.CostEstimate(flops=0, bytes_accessed=4 * math.prod(shape), transcendentals=0),
+    )(*arrays)
+
+
+def pack_down1(own, first):
+    rows = (0, own.shape[1])
+    moves = []
+    at = 0
+    for branch in (2, 3, 4):
+        size = LANES0[branch][1]
+        for source in (0, 1):
+            moves.append((source, (2, 2), rows, LANES0[branch], (0, 2), (at, size)))
+            at += size
+    return pack("pack_down1", (own, first), moves, (2, rows[1], 896))
+
+
+def pack_down2(own, first, second):
+    rows = (0, own.shape[1])
+    moves = []
+    at = 0
     for branch in (3, 4):
-        for array in (own, first):
-            start, size = LANES0[branch]
-            pieces.append(array[1:2, :, start : start + size])
-        start, size = LANES1[branch]
-        pieces.append(second[1:2, :, start : start + size])
-    return cat(*pieces)
-
-
-def step3_rows(own, first, second, third):
-    rows = slice(HEAD_DIM, QKV)
-    return cat(
-        own[0:1, rows, 896:960], first[0:1, rows, 896:960], second[0:1, rows, 768:896], third[0:1, rows, 512:768]
-    )
-
-
-def send_down(own, copy_last):
-    first = partner(own[4:8, :, :960], "row", 0)
-    second = partner(step1_rows(own, first), "row", 1)
-    third = partner(step2_rows(own, first, second), "row", 2)
-    parts = [own, first, second, third]
-    if copy_last:
-        parts.append(partner(step3_rows(*parts), "row", 3))
-    return parts
-
-
-def send_up(out1, out2, out3, out4):
-    third = partner(cat(out3[:, :, 512:1024], out4[:, :, 256:512]), "row", 2)
-
-    def joined(low, high):
-        return jnp.concatenate([low, high], axis=0)
-
-    second = partner(
-        cat(
-            out2[:, :, 512:1024],
-            joined(out3[:, :, 256:512], third[:, :, 256:512]),
-            joined(out4[:, :, 128:256], third[:, :, 640:768]),
-        ),
-        "row",
-        1,
-    )
-
-    def rows_of(at):
-        return cat(
-            out1[:, :, 512 * at : 512 * at + 512],
-            joined(out2[:, :, 256 * at : 256 * at + 256], second[:, :, 256 * at : 256 * at + 256]),
-            jnp.concatenate(
-                [
-                    out3[:, :, 128 * at : 128 * at + 128],
-                    third[:, :, 128 * at : 128 * at + 128],
-                    second[:, :, 512 + 128 * at : 640 + 128 * at],
-                ],
-                axis=0,
-            ),
-            jnp.concatenate(
-                [
-                    out4[:, :, 64 * at : 64 * at + 64],
-                    third[:, :, 512 + 64 * at : 576 + 64 * at],
-                    second[:, :, 768 + 64 * at : 832 + 64 * at],
-                ],
-                axis=0,
-            ),
-        )
-
-    first = partner(rows_of(1), "row", 0)
-    return joined(rows_of(0), first)
+        for source, lanes in ((0, LANES0[branch]), (1, LANES0[branch]), (2, LANES1[branch])):
+            moves.append((source, (1, 1), rows, lanes, (0, 1), (at, lanes[1])))
+            at += lanes[1]
+    return pack("pack_down2", (own, first, second), moves, (1, rows[1], 768))
+
+
+def pack_down3(own, first, second, third):
+    rows = (HEAD_DIM, 2 * HEAD_DIM)
+    moves = []
+    at = 0
+    for source, lanes in ((0, LANES0[4]), (1, LANES0[4]), (2, LANES1[4]), (3, LANES2[4])):
+        moves.append((source, (0, 1), rows, lanes, (0, 1), (at, lanes[1])))
+        at += lanes[1]
+    return pack("pack_down3", (own, first, second, third), moves, (1, rows[1], 512))
+
+
+def pack_up2(out3, out4):
+    rows = (0, out3.shape[1])
+    moves = [(0, (0, 1), rows, (512, 512), (0, 1), (0, 512)), (1, (0, 1), rows, (256, 256), (0, 1), (512, 256))]
+    return pack("pack_up2", (out3, out4), moves, (1, rows[1], 768))
+
+
+def pack_up1(out2, out3, out4, third):
+    rows = (0, out3.shape[1])
+    moves = [
+        (0, (0, 2), rows, (512, 512), (0, 2), (0, 512)),
+        (1, (0, 1), rows, (256, 256), (0, 1), (512, 256)),
+        (3, (0, 1), rows, (256, 256), (1, 1), (512, 256)),
+        (2, (0, 1), rows, (128, 128), (0, 1), (768, 128)),
+        (3, (0, 1), rows, (640, 128), (1, 1), (768, 128)),
+    ]
+    return pack("pack_up1", (out2, out3, out4, third), moves, (2, rows[1], 896))
+
+
+def pack_up0(out1, out2, out3, out4, third, second):
+    rows = (0, out3.shape[1])
+    moves = [
+        (0, (0, 4), rows, (512, 512), (0, 4), (0, 512)),
+        (1, (0, 2), rows, (256, 256), (0, 2), (512, 256)),
+        (5, (0, 2), rows, (256, 256), (2, 2), (512, 256)),
+        (2, (0, 1), rows, (128, 128), (0, 1), (768, 128)),
+        (4, (0, 1), rows, (128, 128), (1, 1), (768, 128)),
+        (5, (0, 2), rows, (640, 128), (2, 2), (768, 128)),
+        (3, (0, 1), rows, (64, 64), (0, 1), (896, 64)),
+        (4, (0, 1), rows, (576, 64), (1, 1), (896, 64)),
+        (5, (0, 2), rows, (832, 64), (2, 2), (896, 64)),
+    ]
+    return pack("pack_up0", (out1, out2, out3, out4, third, second), moves, (4, rows[1], 960))
+
+
+def after(value, *others):
+    return lax.optimization_barrier((value,) + others)[0]
 
 
 def sum_rows(value):
@@ -975,24 +1047,6 @@
     for bit in range(4):
         value = value + partner(value, "row", bit)
     return value
-
-
-def branch_tags(doc_ids, valid, place, unit):
-    tags = jnp.where(valid == 1, doc_ids + 1, 0).reshape(16, 64, 2, 2, 2, 2)
-    tags = tags.transpose(0, 5, 4, 3, 2, 1).reshape(16, SEG0)
-    tags = jnp.take(tags, jnp.arange(16, dtype=jnp.int32) ^ place, axis=0)
-    bit0, bit1, bit2 = place & 1, place >> 1 & 1, place >> 2 & 1
-    dl = 4 * bit0 + 2 * bit1 + bit2
-    result = [jnp.broadcast_to(tags[0][None, None], (8, 1, SEG0))]
-    for branch in range(1, 5):
-        rows = []
-        size = SEG0 >> branch
-        for relative in range(8 >> min(branch, 3)):
-            group = (8 * unit + (relative ^ dl)) % 2**branch
-            start = bitrev(group, branch) * size
-            rows.append(lax.dynamic_slice(tags[: 2**branch], (0, start), (2**branch, size)).reshape(1, SEG0))
-        result.append(jnp.stack(rows))
-    return result, dl
 
 
 def local(
@@ -1020,18 +1074,31 @@
     scaling = HEAD_DIM**-0.5
     unit = lax.axis_index("unit")
     row = lax.axis_index("row")
-    tags, dl = branch_tags(doc_ids, valid, row, unit)
-    place = jnp.stack([dl, unit]).astype(jnp.int32)
-
-    everything, sent, normed_t = project_call(
-        place, tokens, ln1_gain, ln1_shift, w_query, b_query, w_key, w_value, b_value
-    )
-    parts = send_down(sent, True)
+    dl = 4 * (row & 1) + 2 * (row >> 1 & 1) + (row >> 2 & 1)
+    place = jnp.stack([dl, unit, row]).astype(jnp.int32)
+
+    everything, own, away, normed_t, *tags = project_call(
+        place, tokens, doc_ids, valid, ln1_gain, ln1_shift, w_query, b_query, w_key, w_value, b_value
+    )
+    first = partner(away, "row", 0)
     out0, lse0 = forward_call(0, [everything], tags[0])
-    outs = [forward_call(branch, parts, tags[branch])[0] for branch in range(1, 5)]
-    back = send_up(*outs)
-    merged_t, total = merge_call(place, out0, lse0, back)
-    merged_low = merged_t.astype(BF16)
+    first = after(first, out0)
+    second = partner(pack_down1(own, first), "row", 1)
+    out1 = forward_call(1, [own, first], tags[1])[0]
+    second = after(second, out1)
+    third = partner(pack_down2(own, first, second), "row", 2)
+    out2 = forward_call(2, [own, first, second], tags[2])[0]
+    third = after(third, out2)
+    fourth = partner(pack_down3(own, first, second, third), "row", 3)
+    parts = [own, first, second, third, fourth]
+    out3 = forward_call(3, parts, tags[3])[0]
+    out4 = forward_call(4, parts, tags[4])[0]
+    up_third = partner(pack_up2(out3, out4), "row", 2)
+    up_second = partner(pack_up1(out2, out3, out4, up_third), "row", 1)
+    up_first = partner(pack_up0(out1, out2, out3, out4, up_third, up_second), "row", 0)
+    merged_t, merged_low, total = merge_call(
+        place, out0, lse0, (out1, out2, out3, out4, up_third, up_second, up_first)
+    )
 
     order = one_hot_rows(True)
     residual = jnp.dot(order, tokens, preferred_element_type=F32)
@@ -1066,21 +1133,31 @@
     grad_w_out = jnp.dot(merged_low, attention_grad, preferred_element_type=F32)
     merged_grad = lax.dot_general(w_out, attention_grad, NT, preferred_element_type=F32).astype(BF16)
 
-    grad_w_up, grad_w_down, grad_w_out = lax.psum(
-        (grad_w_up.astype(BF16), grad_w_down.astype(BF16), grad_w_out.astype(BF16)), "row"
-    )
-
-    grads_all, grads_sent = spread_call(place, merged_grad, merged_t, total)
-    grad_parts = send_down(grads_sent, False)
-    own_grads = backward_call(0, [everything], [grads_all], tags[0])[0]
-    back1, back2, back3 = [backward_call(b, parts, grad_parts, tags[b])[0] for b in (1, 2, 3)]
+    sums_in = (grad_w_up.astype(BF16), grad_w_down.astype(BF16), grad_w_out.astype(BF16))
+    grad_w_up, grad_w_down, grad_w_out = lax.psum(sums_in, "row")
+
+    merged_grad = after(merged_grad, *sums_in)
+    grads_all, own_grad, away_grad = spread_call(place, merged_grad, merged_t, total)
+    first_grad = partner(away_grad, "row", 0)
+    main0 = backward_call(0, [everything], [grads_all], tags[0])[0]
+    first_grad = after(first_grad, main0)
+    second_grad = partner(pack_down1(own_grad, first_grad), "row", 1)
+    back1 = backward_call(1, parts, [own_grad, first_grad], tags[1])[0]
+    second_grad = after(second_grad, back1)
+    third_grad = partner(pack_down2(own_grad, first_grad, second_grad), "row", 2)
+    grad_parts = [own_grad, first_grad, second_grad, third_grad]
+    back2 = backward_call(2, parts, grad_parts, tags[2])[0]
+    grad_parts[3] = after(third_grad, back2)
     back4, back4_kv = backward_call(4, parts, grad_parts, tags[4])
     other_kv = partner(back4_kv, "row", 3)
+    back3 = backward_call(3, parts, grad_parts, tags[3])[0]
     back4 = jnp.concatenate(
         [back4[:, :HEAD_DIM], (back4[:, HEAD_DIM:].astype(F32) + other_kv.astype(F32)).astype(BF16)], axis=1
     )
-    grads_back = send_up(back1, back2, back3, back4)
-    qkv_grad = collect_call(place, own_grads, grads_back)
+    up_third = partner(pack_up2(back3, back4), "row", 2)
+    up_second = partner(pack_up1(back2, back3, back4, up_third), "row", 1)
+    up_first = partner(pack_up0(back1, back2, back3, back4, up_third, up_second), "row", 0)
+    qkv_grad = collect_call(place, main0, (back1, back2, back3, back4, up_third, up_second, up_first))
     query_grad, key_grad, value_grad = (qkv_grad[at * width : (at + 1) * width] for at in range(3))
 
     grad_w_qkv = lax.dot_general(normed_t, qkv_grad, NT, preferred_element_type=F32)

time: 569 us -> 534 us (0.938)
  local copies, waits for them, and re-layouts: 85.5 us -> 19.4 us
  Pallas kernels: 117 us -> 144 us
  waiting for transfers between devices: 204 us -> 216 us
  other arithmetic: 36.9 us -> 26.2 us
    slice x66 -> x0, local copies, waits for them, and re-layouts: 36.9 us -> none  [the longest x12 9.06 us: step1_rows(): array[2:4, :, start:start + size]]
    pallas_call x4 -> x15, Pallas kernels: 24.2 us -> 51.6 us  [the longest x4 27.9 us: whole_call(): pl.pallas_call(kernel, grid_spec=pltpu.PrefetchScalarGridSpec(num_scalar_...]
    ppermute x26, waiting for transfers between devices: 55.2 us -> 67.2 us  [partner(): return lax.ppermute(value, axis, pairs)]
    reshape x2 -> x0, local copies, waits for them, and re-layouts: 10.5 us -> none  [the longest x1 8.77 us: branch_tags(): tags = jnp.where(valid == 1, doc_ids + 1, 0).reshape(16, 64, 2, 2, 2, 2)]
    concatenate x9 -> x0, other arithmetic: 7.15 us -> none  [the longest x2 5.17 us: joined(): return jnp.concatenate([low, high], axis=0)]
    unnamed x147 -> x127, local copies, waits for them, and re-layouts: 8.61 us -> 15.6 us
    transpose x1 -> x0, local copies, waits for them, and re-layouts: 6.35 us -> none  [branch_tags(): tags = tags.transpose(0, 5, 4, 3, 2, 1).reshape(16, SEG0)]
    broadcast_in_dim x5 -> x0, local copies, waits for them, and re-layouts: 6.25 us -> none  [the longest x1 1.47 us: project_call(): b_query[:, None]]
  transfers between devices with their start and end apart: 31 -> 31, of which waited for: 14 -> 15; matrix products, arithmetic and copies ran while one was open for 25% -> 13% of each run, Pallas kernels for 18% -> 18%
where the time goes in v2:
time: 534 us; the launch traced here: 525 us
  waiting for transfers between devices  216 us (40%)
  Pallas kernels  144 us (27%)
  matrix products  68.9 us (13%)
  starting transfers between devices  35.8 us (7%)
  other arithmetic  26.2 us (5%)
  local copies, waits for them, and re-layouts  19.4 us (4%)
  between operations  15.5 us (3%)
    psum x1, waiting for transfers between devices, local(): grad_w_up, grad_w_down, grad_w_out = lax.psum(sums_in, 'row')  99.9 us
    ppermute x26, waiting for transfers between devices, partner(): return lax.ppermute(value, axis, pairs)  67.2 us
    pallas_call x5, Pallas kernels, backward_call(): pl.pallas_call(partial(backward_kernel, sizes=tuple((piece[2] for piece i...  52.7 us
    ppermute x4, waiting for transfers between devices, swap_unit(): return lax.ppermute(value, 'unit', [(0, 1), (1, 0)])  49 us
    pallas_call x5, Pallas kernels, forward_call(): pl.pallas_call(partial(forward_kernel, sizes=tuple((piece[2] for piece in...  39.3 us
    ppermute x26, starting transfers between devices, partner(): return lax.ppermute(value, axis, pairs)  31.8 us
    pallas_call x4, Pallas kernels, whole_call(): pl.pallas_call(kernel, grid_spec=pltpu.PrefetchScalarGridSpec(num_scalar_...  27.9 us
    pallas_call x11, Pallas kernels, pack(): pl.pallas_call(partial(copy_kernel, moves=moves), out_shape=out, name=nam...  23.8 us
  transfers between devices with their start and end apart: 31, of which 15 were waited for; matrix products, arithmetic and copies ran while one was open for 13% of the time, Pallas kernels for 18%

profile of v2, /device:TPU:1, one launch (start us, length us, event | category | flops | bytes accessed | tf_op | source)
XLA Modules:
  0.0 525.4 jit_solution(13496854922818877945)
XLA Ops:
  7.9 12.1 %project.1 = (bf16[8,144,1024]{2,1,0:T(8,128)(2,1)}, bf16[4,144,960]{2,1,0:T(8,128)(2,1)}, bf16[4,144,960]{2,1,0:T(8,128)(2,1)}, bf16[768,1024]{1,0:T(8,128)(2,1...) custom-call(s32[3]{0:T(128)} %pad_add_fusion.pos_ref, ...), custom_call_target="tpu_custom_call" | custom-call | flops 3422552064 | bytes 9663488 | tf_op jit(solution)/shard_map/project/pallas_call | solution.py:589
  20.0 17.5 %attend0.1 = (f32[8,48,1024]{2,1,0:T(8,128)}, f32[8,1,1024]{2,1,0:T(1,128)}) custom-call(bf16[8,144,1024]{2,1,0:T(8,128)(2,1)} %get-tuple-element.43.refs_0_, s32[1,1024]{1,0:T(1,128)} %get-tuple-element.44.refs_1_.refs_2_), custom_call_target="tpu_custom_call" | custom-call | flops 8589934592 | bytes 4194304 | tf_op jit(solution)/shard_map/attend0/pallas_call | solution.py:771
  43.7 9.6 %attend1.1.refs_0_.out1 = bf16[4,64,1024]{2,1,0:T(8,128)(2,1)} custom-call(bf16[4,144,960]{2,1,0:T(8,128)(2,1)} %get-tuple-element.47.refs_0_, bf16[4,144,960]{2,1,0:T(8,128)(2,1)} %copy-done.3, s32[4,1,1024]{2,1,0:T(1,128)} %get-tuple-element.50.refs_2_.refs_4_), custom_call_target="tpu_custom_call" | custom-call | flops 4294967296 | bytes 2097152 | tf_op jit(solution)/shard_map/attend1/pallas_call | solution.py:771
  60.7 5.8 %attend2.1.refs_0_.refs_1_.out2 = bf16[2,64,1024]{2,1,0:T(8,128)(2,1)} custom-call(bf16[4,144,960]{2,1,0:T(8,128)(2,1)} %get-tuple-element.47.refs_0_, bf16[4,144,960]{2,1,0:T(8,128)(2,1)} %copy-done.3, bf16[2,144,896]{2,1,0:T(8,128)(2,1)} %copy-done.10, s32[2,1,1024]{2,1,0:T(1,128)} %get-tuple-element.52.refs_3_.refs_6_), custom_call_target="tpu_custom_call" | custom-call | flops 2147483648 | bytes 1048576 | tf_op jit(solution)/shard_map/attend2/pallas_call | solution.py:771
  102.1 4.7 merge.1
  119.1 25.6 %collective-permute-done.7 = bf16[1024,768]{0,1:T(8,128)(2,1)S(1)} collective-permute-done((bf16[1024,768]{0,1:T(8,128)(2,1)S(1)}, bf16[1024,768]{0,1:T(8,128)(2,1)S(1)}, u32[]{:S(2)}, u32[]{:S(2)}) %collective-permute-start.7) | collective-permute-done | bytes 1572896 | tf_op jit(solution)/shard_map/ppermute | solution.py:935
  151.5 9.2 %convert_reduce_fusion = (f32[1536]{0:T(1024)}, bf16[1024,1536]{1,0:T(8,128)(2,1)S(1)}) fusion(f32[1024,1536]{1,0:T(8,128)S(1)} %fusion.96, f32[1536]{0:T(1024)S(1)} %copy-done.56, bf16[1024,768]{0,1:T(8,128)(2,1)S(1)} %convolution_convert_fusion.5, bf16[1536,768]{1,0:T(8,128)(2,1)S(1)} %copy-done), kind=kOutput, calls=%fused_computation.18 | convolution fusion | flops 2458384896 | bytes 13381632 | tf_op jit(solution)/shard_map/dot_general | solution.py:1118
  168.8 5.9 %convolution_convert_fusion = bf16[1536,768]{1,0:T(8,128)(2,1)} fusion(bf16[1024,768]{0,1:T(8,128)(2,1)S(1)} %convolution_convert_fusion.5, f32[1024,1536]{1,0:T(8,128)S(1)} %fusion.96, f32[1536]{0:T(1024)S(1)} %copy-done.56), kind=kOutput, calls=%fused_computation.49 | convolution fusion | flops 2432827392 | bytes 10229760 | tf_op jit(solution)/shard_map/dot_general | solution.py:1125
  174.7 23.4 %collective-permute-done.9 = bf16[1024,768]{0,1:T(8,128)(2,1)S(1)} collective-permute-done((bf16[1024,768]{0,1:T(8,128)(2,1)S(1)}, bf16[1024,768]{0,1:T(8,128)(2,1)S(1)}, u32[]{:S(2)}, u32[]{:S(2)}) %collective-permute-start.9) | collective-permute-done | bytes 1572896 | tf_op jit(solution)/shard_map/ppermute | solution.py:935
  208.3 4.6 spread.1
  215.1 24.3 %attend_back0.1.grad_ref = f32[8,144,1024]{2,1,0:T(8,128)} custom-call(bf16[8,144,1024]{2,1,0:T(8,128)(2,1)} %get-tuple-element.43.refs_0_, bf16[8,64,1024]{2,1,0:T(8,128)(2,1)} %get-tuple-element.60.refs_1_, s32[1,1024]{1,0:T(1,128)} %get-tuple-element.44.refs_1_.refs_2_), custom_call_target="tpu_custom_call" | custom-call | flops 12884901888 | bytes 8388608 | tf_op jit(solution)/shard_map/attend_back0/pallas_call | solution.py:795
  243.3 13.0 %attend_back1.1.refs_0_.out1 = bf16[4,144,1024]{2,1,0:T(8,128)(2,1)} custom-call(bf16[4,144,960]{2,1,0:T(8,128)(2,1)} %get-tuple-element.47.refs_0_, bf16[4,144,960]{2,1,0:T(8,128)(2,1)} %copy-done.3, bf16[4,64,960]{2,1,0:T(8,128)(2,1)} %get-tuple-element.61.refs_2_.refs_0_.refs_3_.refs_4_.refs_5_, bf16[4,64,960]{2,1,0:T(8,128)(2,1)} %copy-done.11, ...), custom_call_target="tpu_custom_call" | custom-call | flops 6442450944 | bytes 4194304 | tf_op jit(solution)/shard_map/attend_back1/pallas_call | solution.py:795
  259.1 7.6 %attend_back2.1.refs_0_.refs_1_.out2 = bf16[2,144,1024]{2,1,0:T(8,128)(2,1)} custom-call(bf16[4,144,960]{2,1,0:T(8,128)(2,1)} %get-tuple-element.47.refs_0_, bf16[4,144,960]{2,1,0:T(8,128)(2,1)} %copy-done.3, bf16[2,144,896]{2,1,0:T(8,128)(2,1)} %copy-done.10, bf16[4,64,960]{2,1,0:T(8,128)(2,1)} %get-tuple-element.61.refs_2_.refs_0_.refs_3_.refs_4_.refs_5_, ...), custom_call_target="tpu_custom_call" | custom-call | flops 3221225472 | bytes 2097152 | tf_op jit(solution)/shard_map/attend_back2/pallas_call | solution.py:795
  281.7 6.0 %collective-permute-done.14.refs_3_.refs_4_.third = bf16[1,144,768]{2,1,0:T(8,128)(2,1)S(1)} collective-permute-done((bf16[1,144,768]{2,1,0:T(8,128)(2,1)}, bf16[1,144,768]{2,1,0:T(8,128)(2,1)S(1)}, u32[]{:S(2)}, u32[]{:S(2)}) %collective-permute-start.14) | collective-permute-done | bytes 221216 | tf_op jit(solution)/shard_map/ppermute | solution.py:32
  290.7 11.2 %collective-permute-done.15.refs_5_.second = bf16[2,144,896]{2,1,0:T(8,128)(2,1)S(1)} collective-permute-done((bf16[2,144,896]{2,1,0:T(8,128)(2,1)}, bf16[2,144,896]{2,1,0:T(8,128)(2,1)S(1)}, u32[]{:S(2)}, u32[]{:S(2)}) %collective-permute-start.15) | collective-permute-done | bytes 516128 | tf_op jit(solution)/shard_map/ppermute | solution.py:32
  308.6 7.1 %convolution_convert_fusion.7 = bf16[1024,768]{0,1:T(8,128)(2,1)} fusion(bf16[1536,768]{1,0:T(8,128)(2,1)S(1)} %copy-done, f32[1024,1536]{1,0:T(8,128)} %copy-done.59, f32[1536]{0:T(1024)} %param.34), kind=kOutput, calls=%fused_computation.78 | convolution fusion | flops 2432434176 | bytes 10229760 | tf_op jit(solution)/shard_map/dot_general | solution.py:1122
  317.9 6.4 %collect.1 = bf16[1152,1024]{1,0:T(8,128)(2,1)} custom-call(s32[3]{0:T(128)} %pad_add_fusion.pos_ref, f32[8,144,1024]{2,1,0:T(8,128)} %attend_back0.1.grad_ref, bf16[4,144,1024]{2,1,0:T(8,128)(2,1)} %attend_back1.1.refs_0_.out1, bf16[2,144,1024]{2,1,0:T(8,128)(2,1)} %attend_back2.1.refs_0_.refs_1_.out2, ...), custom_call_target="tpu_custom_call" | custom-call | flops 100000000 | bytes 11132928 | tf_op jit(solution)/shard_map/collect/pallas_call | solution.py:589
  338.6 18.5 %collective-permute-done.23 = bf16[192,1152]{1,0:T(8,128)(2,1)S(1)} collective-permute-done((bf16[192,1152]{1,0:T(8,128)(2,1)S(1)}, bf16[192,1152]{1,0:T(8,128)(2,1)S(1)}, u32[]{:S(2)}, u32[]{:S(2)}) %collective-permute-start.23) | collective-permute-done | bytes 442400 | tf_op jit(solution)/shard_map/ppermute | solution.py:32
  357.4 5.2 convolution_convert_fusion.6
  362.6 99.9 %all-reduce.3.cloned.1.call-done = (bf16[384,768]{1,0:T(8,128)(2,1)}, bf16[768,1536]{1,0:T(8,128)(2,1)}, bf16[1536,768]{1,0:T(8,128)(2,1)}) async-done(((bf16[384,768]{1,0:T(8,128)(2,1)}, bf16[768,1536]{1,0:T(8,128)(2,1)}, bf16[1536,768]{1,0:T(8,128)(2,1)}), (bf16[384,768]{1,0:T(8,128)(2,1)}, bf16[768,1536]{1,0:T(8,128)(2,1)}, bf16[1536,768]{1,0:T(8,128)(2,1)})) %all-reduce.3.cloned.1.call-update) | async-done | bytes 5308432 | tf_op jit(solution)/shard_map/psum | solution.py:1137
  464.7 4.6 convert_element_type.220
  484.8 6.1 %collective-permute-done.26 = bf16[48,1152]{1,0:T(8,128)(2,1)S(1)} collective-permute-done((bf16[48,1152]{1,0:T(8,128)(2,1)S(1)}, bf16[48,1152]{1,0:T(8,128)(2,1)S(1)}, u32[]{:S(2)}, u32[]{:S(2)}) %collective-permute-start.26) | collective-permute-done | bytes 110624 | tf_op jit(solution)/shard_map/ppermute | solution.py:32
  492.5 4.8 collective-permute-done.27
  500.8 6.5 %collective-permute-done.28 = bf16[192,1152]{1,0:T(8,128)(2,1)S(1)} collective-permute-done((bf16[192,1152]{1,0:T(8,128)(2,1)S(1)}, bf16[192,1152]{1,0:T(8,128)(2,1)S(1)}, u32[]{:S(2)}, u32[]{:S(2)}) %collective-permute-start.28) | collective-permute-done | bytes 442400 | tf_op jit(solution)/shard_map/ppermute | solution.py:32
  (259 shorter events, 170.1 us)
Async XLA Ops:
  7.2 455.3 %all-reduce.3.cloned.1.call-start = ((), (), s32[]{:S(2)}) async-start(), calls=%async_computation | async-start | bytes 10616832 | tf_op jit(solution)/shard_map/psum | solution.py:1137
  19.9 17.5 %collective-permute-start = (bf16[4,144,960]{2,1,0:T(8,128)(2,1)}, bf16[4,144,960]{2,1,0:T(8,128)(2,1)S(1)}, u32[]{:S(2)}, u32[]{:S(2)}) collective-permute-start(bf16[4,144,960]{2,1,0:T(8,128)(2,1)} %get-tuple-element.48), channel_id=1, source_target_pairs={{0,1},{1,0},{2,3},{3,2},{4,5},{5,4},{6,7},{7,6},{8,9},{9,8},{10,11... | collective-permute-start | bytes 3317768 | tf_op jit(solution)/shard_map/ppermute | solution.py:32
  41.0 15.0 %collective-permute-start.1 = (bf16[2,144,896]{2,1,0:T(8,128)(2,1)}, bf16[2,144,896]{2,1,0:T(8,128)(2,1)S(1)}, u32[]{:S(2)}, u32[]{:S(2)}) collective-permute-start(bf16[2,144,896]{2,1,0:T(8,128)(2,1)} %pack_down1.2), channel_id=1, source_target_pairs={{0,2},{1,3},{2,0},{3,1},{4,6},{5,7},{6,4},{7,5},{8,10},{9,11},{10,... | collective-permute-start | bytes 1548296 | tf_op jit(solution)/shard_map/ppermute | solution.py:32
  59.3 7.2 %collective-permute-start.2 = (bf16[1,144,768]{2,1,0:T(8,128)(2,1)}, bf16[1,144,768]{2,1,0:T(8,128)(2,1)S(1)}, u32[]{:S(2)}, u32[]{:S(2)}) collective-permute-start(bf16[1,144,768]{2,1,0:T(8,128)(2,1)} %pack_down2.2), channel_id=1, source_target_pairs={{0,4},{1,5},{2,6},{3,7},{4,0},{5,1},{6,2},{7,3},{8,12},{9,13},{10,... | collective-permute-start | bytes 663560 | tf_op jit(solution)/shard_map/ppermute | solution.py:32
  69.7 7.5 %collective-permute-start.3 = (bf16[1,96,512]{2,1,0:T(8,128)(2,1)}, bf16[1,96,512]{2,1,0:T(8,128)(2,1)S(1)}, u32[]{:S(2)}, u32[]{:S(2)}) collective-permute-start(bf16[1,96,512]{2,1,0:T(8,128)(2,1)} %pack_down3.1), channel_id=1, source_target_pairs={{0,8},{1,9},{2,10},{3,11},{4,12},{5,13},{6,14},{7,15},{8,0},{9,1},... | collective-permute-start | bytes 294920 | tf_op jit(solution)/shard_map/ppermute | solution.py:32
  109.0 35.7 %collective-permute-start.7 = (bf16[1024,768]{0,1:T(8,128)(2,1)S(1)}, bf16[1024,768]{0,1:T(8,128)(2,1)S(1)}, u32[]{:S(2)}, u32[]{:S(2)}) collective-permute-start(bf16[1024,768]{0,1:T(8,128)(2,1)S(1)} %convolution_convert_fusion.3), channel_id=1, source_target_pairs={{0,16},{16,0},{1,17},{17,1},{2,18},{18,2},{3,19},{19,3},{4,20},{20... | collective-permute-start | bytes 4718600 | tf_op jit(solution)/shard_map/ppermute | solution.py:935
  163.4 34.7 %collective-permute-start.9 = (bf16[1024,768]{0,1:T(8,128)(2,1)S(1)}, bf16[1024,768]{0,1:T(8,128)(2,1)S(1)}, u32[]{:S(2)}, u32[]{:S(2)}) collective-permute-start(bf16[1024,768]{0,1:T(8,128)(2,1)S(1)} %convolution_convert_fusion.4), channel_id=1, source_target_pairs={{0,16},{16,0},{1,17},{17,1},{2,18},{18,2},{3,19},{19,3},{4,20},{20... | collective-permute-start | bytes 4718600 | tf_op jit(solution)/shard_map/ppermute | solution.py:935
  212.9 26.5 %collective-permute-start.10 = (bf16[4,64,960]{2,1,0:T(8,128)(2,1)}, bf16[4,64,960]{2,1,0:T(8,128)(2,1)S(1)}, u32[]{:S(2)}, u32[]{:S(2)}) collective-permute-start(bf16[4,64,960]{2,1,0:T(8,128)(2,1)} %get-tuple-element.62), channel_id=1, source_target_pairs={{0,1},{1,0},{2,3},{3,2},{4,5},{5,4},{6,7},{7,6},{8,9},{9,8},{10,11... | collective-permute-start | bytes 1474568 | tf_op jit(solution)/shard_map/ppermute | solution.py:32
  242.2 14.2 %collective-permute-start.11 = (bf16[2,64,896]{2,1,0:T(8,128)(2,1)}, bf16[2,64,896]{2,1,0:T(8,128)(2,1)S(1)}, u32[]{:S(2)}, u32[]{:S(2)}) collective-permute-start(bf16[2,64,896]{2,1,0:T(8,128)(2,1)} %pack_down1.3), channel_id=1, source_target_pairs={{0,2},{1,3},{2,0},{3,1},{4,6},{5,7},{6,4},{7,5},{8,10},{9,11},{10,... | collective-permute-start | bytes 688136 | tf_op jit(solution)/shard_map/ppermute | solution.py:32
  259.0 7.6 %collective-permute-start.12 = (bf16[1,64,768]{2,1,0:T(8,128)(2,1)}, bf16[1,64,768]{2,1,0:T(8,128)(2,1)S(1)}, u32[]{:S(2)}, u32[]{:S(2)}) collective-permute-start(bf16[1,64,768]{2,1,0:T(8,128)(2,1)} %pack_down2.3), channel_id=1, source_target_pairs={{0,4},{1,5},{2,6},{3,7},{4,0},{5,1},{6,2},{7,3},{8,12},{9,13},{10,... | collective-permute-start | bytes 294920 | tf_op jit(solution)/shard_map/ppermute | solution.py:32
  271.4 7.9 %collective-permute-start.13 = (bf16[1,96,512]{2,1,0:T(8,128)(2,1)}, bf16[1,96,512]{2,1,0:T(8,128)(2,1)S(1)}, u32[]{:S(2)}, u32[]{:S(2)}) collective-permute-start(bf16[1,96,512]{2,1,0:T(8,128)(2,1)} %get-tuple-element.67), channel_id=1, source_target_pairs={{0,8},{1,9},{2,10},{3,11},{4,12},{5,13},{6,14},{7,15},{8,0},{9,1},... | collective-permute-start | bytes 294920 | tf_op jit(solution)/shard_map/ppermute | solution.py:32
  290.5 11.4 %collective-permute-start.15 = (bf16[2,144,896]{2,1,0:T(8,128)(2,1)}, bf16[2,144,896]{2,1,0:T(8,128)(2,1)S(1)}, u32[]{:S(2)}, u32[]{:S(2)}) collective-permute-start(bf16[2,144,896]{2,1,0:T(8,128)(2,1)} %pack_up1.3), channel_id=1, source_target_pairs={{0,2},{1,3},{2,0},{3,1},{4,6},{5,7},{6,4},{7,5},{8,10},{9,11},{10,... | collective-permute-start | bytes 1548296 | tf_op jit(solution)/shard_map/ppermute | solution.py:32
  305.6 11.2 %collective-permute-start.16 = (bf16[4,144,960]{2,1,0:T(8,128)(2,1)}, bf16[4,144,960]{2,1,0:T(8,128)(2,1)S(1)}, u32[]{:S(2)}, u32[]{:S(2)}) collective-permute-start(bf16[4,144,960]{2,1,0:T(8,128)(2,1)} %pack_up0.3), channel_id=1, source_target_pairs={{0,1},{1,0},{2,3},{3,2},{4,5},{5,4},{6,7},{7,6},{8,9},{9,8},{10,11... | collective-permute-start | bytes 3317768 | tf_op jit(solution)/shard_map/ppermute | solution.py:32
  315.7 41.6 %collective-permute-start.8 = (bf16[1024,768]{0,1:T(8,128)(2,1)}, bf16[1024,768]{0,1:T(8,128)(2,1)}, u32[]{:S(2)}, u32[]{:S(2)}) collective-permute-start(bf16[1024,768]{0,1:T(8,128)(2,1)} %convolution_convert_fusion.7), channel_id=1, source_target_pairs={{0,16},{16,0},{1,17},{17,1},{2,18},{18,2},{3,19},{19,3},{4,20},{20... | collective-permute-start | bytes 4718600 | tf_op jit(solution)/shard_map/ppermute | solution.py:935
  335.7 21.3 %collective-permute-start.23 = (bf16[192,1152]{1,0:T(8,128)(2,1)S(1)}, bf16[192,1152]{1,0:T(8,128)(2,1)S(1)}, u32[]{:S(2)}, u32[]{:S(2)}) collective-permute-start(bf16[192,1152]{1,0:T(8,128)(2,1)S(1)} %constant_dynamic-slice_fusion.2), channel_id=1, source_target_pairs={{0,2},{1,3},{2,0},{3,1},{4,6},{5,7},{6,4},{7,5},{8,10},{9,11},{10,... | collective-permute-start | bytes 1327112 | tf_op jit(solution)/shard_map/ppermute | solution.py:32
  338.4 136.2 %collective-permute-start.17 = (bf16[1024,768]{0,1:T(8,128)(2,1)}, bf16[1024,768]{0,1:T(8,128)(2,1)}, u32[]{:S(2)}, u32[]{:S(2)}) collective-permute-start(bf16[1024,768]{0,1:T(8,128)(2,1)} %add_convert_fusion), channel_id=1, source_target_pairs={{0,16},{16,0},{1,17},{17,1},{2,18},{18,2},{3,19},{19,3},{4,20},{20... | collective-permute-start | bytes 4718600 | tf_op jit(solution)/shard_map/ppermute | solution.py:935
  357.2 115.1 %collective-permute-start.24 = (bf16[96,1152]{1,0:T(8,128)(2,1)S(1)}, bf16[96,1152]{1,0:T(8,128)(2,1)S(1)}, u32[]{:S(2)}, u32[]{:S(2)}) collective-permute-start(bf16[96,1152]{1,0:T(8,128)(2,1)S(1)} %constant_dynamic-slice_fusion.1), channel_id=1, source_target_pairs={{0,4},{1,5},{2,6},{3,7},{4,0},{5,1},{6,2},{7,3},{8,12},{9,13},{10,... | collective-permute-start | bytes 663560 | tf_op jit(solution)/shard_map/ppermute | solution.py:32
  472.5 10.1 %collective-permute-start.25 = (bf16[48,1152]{1,0:T(8,128)(2,1)S(1)}, bf16[48,1152]{1,0:T(8,128)(2,1)S(1)}, u32[]{:S(2)}, u32[]{:S(2)}) collective-permute-start(bf16[48,1152]{1,0:T(8,128)(2,1)S(1)} %constant_dynamic-slice_fusion), channel_id=1, source_target_pairs={{0,8},{1,9},{2,10},{3,11},{4,12},{5,13},{6,14},{7,15},{8,0},{9,1},... | collective-permute-start | bytes 331784 | tf_op jit(solution)/shard_map/ppermute | solution.py:32
  482.6 8.2 %collective-permute-start.26 = (bf16[48,1152]{1,0:T(8,128)(2,1)S(1)}, bf16[48,1152]{1,0:T(8,128)(2,1)S(1)}, u32[]{:S(2)}, u32[]{:S(2)}) collective-permute-start(bf16[48,1152]{1,0:T(8,128)(2,1)S(1)} %add_convert_fusion.7), channel_id=1, source_target_pairs={{0,8},{1,9},{2,10},{3,11},{4,12},{5,13},{6,14},{7,15},{8,0},{9,1},... | collective-permute-start | bytes 331784 | tf_op jit(solution)/shard_map/ppermute | solution.py:32
  483.5 7.5 %collective-permute-start.19 = (f32[54,128]{1,0:T(8,128)S(1)}, f32[54,128]{1,0:T(8,128)S(1)}, u32[]{:S(2)}, u32[]{:S(2)}) collective-permute-start(f32[54,128]{1,0:T(8,128)S(1)} %bitcast_add_fusion), channel_id=1, source_target_pairs={{0,2},{1,3},{2,0},{3,1},{4,6},{5,7},{6,4},{7,5},{8,10},{9,11},{10,... | collective-permute-start | bytes 82952 | tf_op jit(solution)/shard_map/ppermute | solution.py:32
  491.0 9.7 %collective-permute-start.20 = (f32[54,128]{1,0:T(8,128)S(1)}, f32[54,128]{1,0:T(8,128)S(1)}, u32[]{:S(2)}, u32[]{:S(2)}) collective-permute-start(f32[54,128]{1,0:T(8,128)S(1)} %fusion.127), channel_id=1, source_target_pairs={{0,4},{1,5},{2,6},{3,7},{4,0},{5,1},{6,2},{7,3},{8,12},{9,13},{10,... | collective-permute-start | bytes 82952 | tf_op jit(solution)/shard_map/ppermute | solution.py:32
  497.4 10.0 %collective-permute-start.28 = (bf16[192,1152]{1,0:T(8,128)(2,1)S(1)}, bf16[192,1152]{1,0:T(8,128)(2,1)S(1)}, u32[]{:S(2)}, u32[]{:S(2)}) collective-permute-start(bf16[192,1152]{1,0:T(8,128)(2,1)S(1)} %maximum_select_fusion.2), channel_id=1, source_target_pairs={{0,2},{1,3},{2,0},{3,1},{4,6},{5,7},{6,4},{7,5},{8,10},{9,11},{10,... | collective-permute-start | bytes 1327112 | tf_op jit(solution)/shard_map/ppermute | solution.py:32
  500.7 13.3 %collective-permute-start.21 = (f32[54,128]{1,0:T(8,128)S(1)}, f32[54,128]{1,0:T(8,128)S(1)}, u32[]{:S(2)}, u32[]{:S(2)}) collective-permute-start(f32[54,128]{1,0:T(8,128)S(1)} %add.265), channel_id=1, source_target_pairs={{0,8},{1,9},{2,10},{3,11},{4,12},{5,13},{6,14},{7,15},{8,0},{9,1},... | collective-permute-start | bytes 82952 | tf_op jit(solution)/shard_map/ppermute | solution.py:32
  507.6 8.3 %collective-permute-start.29 = (bf16[384,1152]{1,0:T(8,128)(2,1)S(1)}, bf16[384,1152]{1,0:T(8,128)(2,1)S(1)}, u32[]{:S(2)}, u32[]{:S(2)}) collective-permute-start(bf16[384,1152]{1,0:T(8,128)(2,1)S(1)} %maximum_select_fusion.1), channel_id=1, source_target_pairs={{0,1},{1,0},{2,3},{3,2},{4,5},{5,4},{6,7},{7,6},{8,9},{9,8},{10,11... | collective-permute-start | bytes 2654216 | tf_op jit(solution)/shard_map/ppermute | solution.py:32
  (67 other events, 822.4 us)
Sparse Core Ops, SparseCore 0:
  331.3 131.1 all-reduce.2
